TPU v7x, 128 devices: a whole 4x4x4 slice. The times are simulated.
128 devices in a mesh: tm: 16 (over y, x), ops: 8 (over z, core).
Axes of the slice: x: 4, y: 4, z: 4, core: 2. Of those that a mesh axis runs over, the one named last changes fastest.
Arguments:
- node_blocks: bfloat16 [512, 384, 768], P(('tm', 'ops')), may hold values from -6 to 6
- first_pulls: int32 [128, 16], replicated, may hold values from 0 to 511, as said below
- first_left: int32 [128, 24], replicated, may hold values from 0 to 15
- first_right: int32 [128, 24], replicated, may hold values from 0 to 15
- first_live: int32 [128], replicated, may hold values from 1 to 24, as said below
- second_pulls: int32 [128, 16], replicated, may hold values from 0 to 3071, as said below
- second_left: int32 [128, 16], replicated, may hold values from 0 to 15
- second_right: int32 [128, 16], replicated, may hold values from 0 to 15
- second_live: int32 [128], replicated, may hold values from 1 to 16, as said below
- diagram_ids: int32 [128, 16], replicated, may hold values from 0 to 127, as said below
- diagram_signs: int32 [128, 16], replicated, may hold values from -1 to 1, as said below
Outputs:
- diagrams: float32 [128, 384, 768], P(('tm', 'ops'))
Inputs may be any that keep to these rules, and one draw needn't show every extreme that they name: `first_pulls`: every node in row w belongs to a device with the same ops index as w. At most 1 entries of a row belong to any one device, and every row has a device with exactly 1. `first_live`: some worker has 24 pairs. `second_pulls`: each entry is an id h * 24 + p with p < first_live[h], where h is a device with the same tm index as w. At most 2 entries of a row belong to any one device h, and every row has a device with exactly 2. `second_live`: some worker has 16 pairs. `diagram_ids`: every diagram of row w is owned by a device with the same tm index as w. `diagram_signs`: each entry is +1 or -1.
All inputs are finite; a program needn't handle non-finite values.
Results may differ from a plain program's by a relative error of at most 0.004.
Values may be sent and summed in bfloat16 or wider, within the bound.
No kernel may reach another device: no remote copies, remote signals or barrier semaphores. Data moves between devices by JAX's collectives and lax.ppermute only.
A program may use at most 128 MiB of HBM per device.

v0:
```python
import math

import jax
import jax.numpy as jnp
from jax import lax
from jax.experimental import pallas as pl
from jax.experimental.pallas import tpu as pltpu
from jax.sharding import PartitionSpec as P


ANY = pl.BlockSpec(memory_space=pl.ANY)
SMEM = pl.BlockSpec(memory_space=pltpu.SMEM)
SIDE = 4
OTHERS = (1, 2, 3)
FAR = ((2, 0), (2, 1))
NEAR = ((1, 0), (1, 1), (3, 0), (3, 1))
HERE = ((0, 1), (0, 0))


def shift_tm(value, dy, dx):
    pairs = [
        (y * SIDE + x, (y + dy) % SIDE * SIDE + (x + dx) % SIDE)
        for y in range(SIDE)
        for x in range(SIDE)
    ]
    return lax.ppermute(value, "tm", pairs)


def shift_ops(value, dz, dc):
    pairs = [
        (z * 2 + core, (z + dz) % SIDE * 2 + (core + dc) % 2)
        for z in range(SIDE)
        for core in range(2)
    ]
    return lax.ppermute(value, "ops", pairs)


def column(table, index):
    return lax.dynamic_slice_in_dim(table.T, index, 1, axis=1)[:, 0]


def look_up(values, keys):
    hits = keys[:, None] == jnp.arange(values.shape[0])[None, :]
    return jnp.sum(jnp.where(hits, values[None, :], 0), axis=1)


def copy_all(copies):
    for copy in copies:
        copy.start()
    for copy in copies:
        copy.wait()


def stack_right(block, stacked, rank):
    stacked[:rank, :] = block
    stacked[rank:, :rank] = -block[:, rank:]
    stacked[rank:, rank:] = block[:, :rank]


def half_shape(nodes, count):
    return jax.ShapeDtypeStruct((count, nodes.shape[1] // 2, nodes.shape[2]), nodes.dtype)


def pick_own(place, wants, nodes):
    half = nodes.shape[1] // 2

    def kernel(place_ref, wants_ref, nodes_ref, *refs):
        outs, sems = refs[:-1], refs[-1]
        y, x = place_ref[0], place_ref[1]
        me = y * SIDE + x
        copies = []
        for n, d in enumerate(OTHERS):
            upper = wants_ref[(y + d) % SIDE * SIDE + x, me]
            lower = wants_ref[y * SIDE + (x + d) % SIDE, me]
            copies.append(
                pltpu.make_async_copy(nodes_ref.at[pl.ds(upper, 1), :half], outs[n], sems.at[n])
            )
            copies.append(
                pltpu.make_async_copy(
                    nodes_ref.at[pl.ds(lower, 1), half:], outs[3 + n], sems.at[3 + n]
                )
            )
        copies.append(
            pltpu.make_async_copy(nodes_ref.at[wants_ref[me, me]], outs[6], sems.at[6])
        )
        copy_all(copies)

    return pl.pallas_call(
        kernel,
        out_shape=[half_shape(nodes, 1)] * 6
        + [jax.ShapeDtypeStruct(nodes.shape[1:], nodes.dtype)],
        in_specs=[SMEM, SMEM, pl.BlockSpec(memory_space=pltpu.VMEM)],
        out_specs=[ANY] * 7,
        scratch_shapes=[pltpu.SemaphoreType.DMA((7,))],
        compiler_params=pltpu.CompilerParams(vmem_limit_bytes=6 << 20),
        name="pick_own",
    )(place, wants, nodes)


def pick_relayed(place, wants, across, along):
    def kernel(place_ref, wants_ref, *refs):
        gathered, outs, sems = refs[:12], refs[12:20], refs[20]
        y, x = place_ref[0], place_ref[1]
        waits = []
        for line in range(2):
            for d in range(SIDE):
                for n, behind in enumerate(OTHERS):
                    if line == 0:
                        reader = (y + d) % SIDE * SIDE + x
                        source = y * SIDE + (x + SIDE - behind) % SIDE
                    else:
                        reader = y * SIDE + (x + d) % SIDE
                        source = (y + SIDE - behind) % SIDE * SIDE + x
                    slot = wants_ref[reader, source]
                    low, high = gathered[(line * 3 + n) * 2], gathered[(line * 3 + n) * 2 + 1]
                    target = outs[line * SIDE + d].at[n]
                    sem = sems.at[(line * SIDE + d) * 3 + n]
                    inner = slot % 2

                    @pl.when(slot < 2)
                    def _(low=low, target=target, sem=sem, inner=inner):
                        pltpu.make_async_copy(low.at[inner], target, sem).start()

                    @pl.when(slot >= 2)
                    def _(high=high, target=target, sem=sem, inner=inner):
                        pltpu.make_async_copy(high.at[inner], target, sem).start()

                    waits.append(pltpu.make_async_copy(low.at[0], target, sem))
        for wait in waits:
            wait.wait()

    arrays = [array for pair in across + along for array in pair]
    shape = jax.ShapeDtypeStruct((3,) + arrays[0].shape[1:], arrays[0].dtype)
    outs = pl.pallas_call(
        kernel,
        out_shape=[shape] * 8,
        in_specs=[SMEM, SMEM] + [pl.BlockSpec(memory_space=pltpu.VMEM)] * 12,
        out_specs=[ANY] * 8,
        scratch_shapes=[pltpu.SemaphoreType.DMA((24,))],
        compiler_params=pltpu.CompilerParams(vmem_limit_bytes=9 << 20),
        name="pick_relayed",
    )(place, wants, *arrays)
    return outs[:4], outs[4:]


def pair_products(left, right, pieces, outputs, norm):
    own, upper, lower = pieces
    rank, width = own.shape
    half = rank // 2
    upper_line, upper_far, lower_line, lower_far = *upper, *lower

    def kernel(left_ref, right_ref, *refs):
        own_ref, rest = refs[0], refs[1:15]
        outs, (blocks, stacked, sems) = refs[15 : 15 + outputs], refs[15 + outputs :]
        step = pl.program_id(0)

        @pl.when(step == 0)
        def _():
            pairs = [(own_ref, blocks.at[0, 0])]
            for n, d in enumerate(OTHERS):
                pairs.append((rest[n], blocks.at[d, pl.ds(0, 1), :half]))
                pairs.append((rest[7 + n], blocks.at[pl.ds(0, 1), d, half:]))
            for d in range(SIDE):
                pairs.append((rest[3 + d], blocks.at[d, pl.ds(1, 3), :half]))
                pairs.append((rest[10 + d], blocks.at[pl.ds(1, 3), d, half:]))
            copy_all(
                [
                    pltpu.make_async_copy(source, target, sems.at[n])
                    for n, (source, target) in enumerate(pairs)
                ]
            )

        for n, out_ref in enumerate(outs):
            a, b = left_ref[n * 2 + step], right_ref[n * 2 + step]
            stack_right(blocks[b // SIDE, b % SIDE], stacked, rank)
            product = jnp.dot(
                blocks[a // SIDE, a % SIDE], stacked[...], preferred_element_type=jnp.float32
            )
            out_ref[...] = (product * norm).astype(out_ref.dtype)

    return pl.pallas_call(
        kernel,
        out_shape=[jax.ShapeDtypeStruct((2, rank, width), jnp.bfloat16)] * outputs,
        grid_spec=pltpu.PrefetchScalarGridSpec(
            num_scalar_prefetch=2,
            grid=(2,),
            in_specs=[ANY] * 15,
            out_specs=[pl.BlockSpec((None, rank, width), lambda i, l, r: (i, 0, 0))] * outputs,
            scratch_shapes=[
                pltpu.VMEM((SIDE, SIDE, rank, width), jnp.bfloat16),
                pltpu.VMEM((width, width), jnp.bfloat16),
                pltpu.SemaphoreType.DMA((15,)),
            ],
        ),
        compiler_params=pltpu.CompilerParams(vmem_limit_bytes=20 << 20),
        name="pair_products",
    )(left, right, own, *upper_line, *upper_far, *lower_line, *lower_far)


def signed_sums(left, right, target, sign, live, pieces, norm):
    rank, width = pieces[0].shape[1:]
    count = len(pieces)

    def kernel(left_ref, right_ref, target_ref, sign_ref, live_ref, *refs):
        keep_ref, give_ref, blocks, stacked, sums, sems = refs[count:]
        copies = [
            pltpu.make_async_copy(refs[n], blocks.at[pl.ds(2 * n, 2)], sems.at[n])
            for n in range(count)
        ]
        for copy in copies:
            copy.start()
        keep_ref[...] = jnp.zeros_like(keep_ref)
        sums[...] = jnp.zeros_like(sums)
        for copy in copies:
            copy.wait()

        def pair(index, carry):
            stack_right(blocks[right_ref[index]], stacked, rank)
            product = jnp.dot(
                blocks[left_ref[index]], stacked[...], preferred_element_type=jnp.float32
            )
            term = product * (sign_ref[index].astype(jnp.float32) * norm)
            where = target_ref[index]

            @pl.when(where < SIDE)
            def _():
                keep_ref[where % SIDE] += term

            @pl.when(where >= SIDE)
            def _():
                sums[where % SIDE] += term

            return carry

        lax.fori_loop(0, live_ref[0], pair, 0)
        give_ref[...] = sums[...].astype(give_ref.dtype)

    return pl.pallas_call(
        kernel,
        out_shape=[
            jax.ShapeDtypeStruct((SIDE, rank, width), jnp.float32),
            jax.ShapeDtypeStruct((SIDE, rank, width), jnp.bfloat16),
        ],
        in_specs=[SMEM] * 5 + [ANY] * count,
        out_specs=[pl.BlockSpec(memory_space=pltpu.VMEM)] * 2,
        scratch_shapes=[
            pltpu.VMEM((2 * count, rank, width), jnp.bfloat16),
            pltpu.VMEM((width, width), jnp.bfloat16),
            pltpu.VMEM((SIDE, rank, width), jnp.float32),
            pltpu.SemaphoreType.DMA((count,)),
        ],
        compiler_params=pltpu.CompilerParams(vmem_limit_bytes=32 << 20),
        name="signed_sums",
    )(left, right, target, sign, live, *pieces)


def gather_nodes(node_blocks, place, wants):
    half = node_blocks.shape[1] // 2
    upper = [node_blocks[:2, :half], node_blocks[2:, :half]]
    lower = [node_blocks[:2, half:], node_blocks[2:, half:]]
    up, down = {}, {}
    for part in range(2):
        up[1, part] = shift_tm(upper[part], 0, 1)
        down[1, part] = shift_tm(lower[part], 1, 0)
        up[3, 1 - part] = shift_tm(upper[1 - part], 0, 3)
        down[3, 1 - part] = shift_tm(lower[1 - part], 3, 0)
    up[2, 0] = shift_tm(up[1, 0], 0, 1)
    down[2, 0] = shift_tm(down[1, 0], 1, 0)
    up[2, 1] = shift_tm(up[3, 1], 0, 3)
    down[2, 1] = shift_tm(down[3, 1], 3, 0)
    picked = pick_own(place, wants, node_blocks)
    upper_line = [shift_tm(picked[n], d, 0) for n, d in enumerate(OTHERS)]
    lower_line = [shift_tm(picked[3 + n], 0, d) for n, d in enumerate(OTHERS)]
    along_y, along_x = pick_relayed(
        place,
        wants,
        [(up[d, 0], up[d, 1]) for d in OTHERS],
        [(down[d, 0], down[d, 1]) for d in OTHERS],
    )
    far_y, far_x = {0: along_y[0]}, {0: along_x[0]}
    for d in (2, 1, 3):
        far_y[d] = shift_tm(along_y[d], d, 0)
        far_x[d] = shift_tm(along_x[d], 0, d)
    upper_far = [far_y[d] for d in range(SIDE)]
    lower_far = [far_x[d] for d in range(SIDE)]
    return picked[6], (upper_line, upper_far), (lower_line, lower_far)


def body(
    node_blocks,
    first_pulls,
    first_left,
    first_right,
    first_live,
    second_pulls,
    second_left,
    second_right,
    second_live,
    diagram_ids,
    diagram_signs,
):
    times = lax.axis_size("tm")
    groups = lax.axis_size("ops")
    time = lax.axis_index("tm")
    group = lax.axis_index("ops")
    worker = time * groups + group
    y, x = time // SIDE, time % SIDE
    z, core = group // 2, group % 2
    held, rank = node_blocks.shape[:2]
    norm = 1.0 / math.sqrt(2.0 * rank)
    cap = first_left.shape[1]
    reads = second_pulls.shape[1]

    pulls = lax.dynamic_slice_in_dim(
        first_pulls.T.reshape(first_pulls.shape[1], times, groups), group, 1, axis=2
    )[:, :, 0]
    from_time = (pulls // (held * groups))[:, :, None] == jnp.arange(times)[None, None, :]
    wants = jnp.sum(jnp.where(from_time, (pulls % held)[:, :, None], 0), axis=0)
    place = jnp.stack([y, x])
    pieces = gather_nodes(node_blocks, place, wants)

    source = column(first_pulls, worker) // (held * groups)
    source = (y - source // SIDE) % SIDE * SIDE + (x - source % SIDE) % SIDE
    pair_left = look_up(source, column(first_left, worker))
    pair_right = look_up(source, column(first_right, worker))
    row_pulls = lax.dynamic_slice_in_dim(second_pulls.T, time * groups, groups, axis=1)
    coded = jnp.arange(reads)[:, None] * 64 + row_pulls % cap
    mine = row_pulls // cap == worker
    first_pair = jnp.min(jnp.where(mine, coded, reads * 64), axis=0) % 64
    last_pair = jnp.max(jnp.where(mine, coded, 0), axis=0) % 64
    offsets = FAR + NEAR + HERE
    readers = (z + jnp.array([dz for dz, _ in offsets])) % SIDE * 2
    readers = readers + (core + jnp.array([dc for _, dc in offsets])) % 2
    wanted = jnp.stack([look_up(first_pair, readers), look_up(last_pair, readers)], axis=1)
    wanted = wanted.reshape(-1)
    left, right = look_up(pair_left, wanted), look_up(pair_right, wanted)
    arrived = {}
    done = 0
    for part in (FAR, NEAR, HERE):
        here = slice(2 * done, 2 * (done + len(part)))
        products = pair_products(left[here], right[here], pieces, len(part), norm)
        for offset, product in zip(part, products):
            arrived[offset] = product if offset == (0, 0) else shift_ops(product, *offset)
        done += len(part)

    source = column(second_pulls, worker) // cap % groups
    earlier = jnp.arange(reads)[:, None] > jnp.arange(reads)[None, :]
    again = jnp.any(jnp.logical_and(source[:, None] == source[None, :], earlier), axis=1)
    offset = (z - source // 2) % SIDE * 2 + (core + source) % 2
    slot = offset * 2 + again.astype(jnp.int32)
    target = column(diagram_ids, worker) - time * groups
    target = (target // 2 - z) % SIDE + (target + core) % 2 * SIDE
    keep, give = signed_sums(
        look_up(slot, column(second_left, worker)),
        look_up(slot, column(second_right, worker)),
        target,
        column(diagram_signs, worker),
        lax.dynamic_slice_in_dim(second_live, worker, 1),
        [arrived[dz, dc] for dz in range(SIDE) for dc in range(2)],
        norm,
    )
    both = keep + shift_ops(give, 0, 1).astype(jnp.float32)
    total = both[0]
    parts = {d: shift_ops(both[d].astype(jnp.bfloat16), d, 0) for d in (2, 1, 3)}
    for d in OTHERS:
        total = total + parts[d].astype(jnp.float32)
    return total[None]


def solution(mesh):
    placed = (P(("tm", "ops"), None, None),) + (P(),) * 10
    return jax.shard_map(body, mesh=mesh, in_specs=placed, out_specs=P(("tm", "ops"), None, None), check_vma=False)
```

profile of v0, /device:TPU:1, one launch (start us, length us, event | category | flops | bytes accessed | tf_op | source)
XLA Modules:
  0.0 307.0 jit_solution(8663813138588569937)
XLA Ops:
  0.0 2.6 fusion.35
  2.6 2.1 collective-permute-start.9
  4.7 1.4 collective-permute-start.12
  6.1 1.2 collective-permute-start.3
  7.3 1.5 collective-permute-start.6
  8.8 10.2 %collective-permute-done.9.refs_6_ = bf16[2,192,768]{2,1,0:T(8,128)(2,1)S(1)} collective-permute-done((bf16[2,192,768]{2,1,0:T(8,128)(2,1)S(1)}, bf16[2,192,768]{2,1,0:T(8,128)(2,1)S(1)}, u32[]{:S(2)}, u32[]{:S(2)}) %collective-permute-start.9) | collective-permute-done | bytes 589856 | tf_op jit(solution)/shard_map/ppermute | solution.py:26
  19.1 1.3 collective-permute-start.14
  20.4 1.2 collective-permute-start.4
  21.6 1.5 collective-permute-start.8
  23.2 8.5 %collective-permute-done.10.refs_7_ = bf16[2,192,768]{2,1,0:T(8,128)(2,1)S(1)} collective-permute-done((bf16[2,192,768]{2,1,0:T(8,128)(2,1)S(1)}, bf16[2,192,768]{2,1,0:T(8,128)(2,1)S(1)}, u32[]{:S(2)}, u32[]{:S(2)}) %collective-permute-start.10) | collective-permute-done | bytes 589856 | tf_op jit(solution)/shard_map/ppermute | solution.py:26
  32.5 1.4 collective-permute-start.13
  34.7 1.2 collective-permute-start.5
  36.8 1.5 collective-permute-start.7
  39.8 1.5 and_select_fusion.1
  42.3 2.1 collective-permute-done.11.refs_8_
  46.0 2.0 collective-permute-done.5.refs_2_
  48.8 1.1 copy-done.25
  49.9 1.1 copy-done.27
  50.9 1.1 copy-done.29
  52.0 1.1 copy-done.31
  53.1 1.1 copy-done.33
  54.1 1.1 copy-done.35
  55.2 3.6 %pick_relayed.1 = (bf16[3,192,768]{2,1,0:T(8,128)(2,1)S(1)}, bf16[3,192,768]{2,1,0:T(8,128)(2,1)}, bf16[3,192,768]{2,1,0:T(8,128)(2,1)S(1)}, bf16[3,192,768]{2,1...) custom-call(s32[2]{0:T(128)S(1)} %pad_add_fusion.1.place_ref, ...), custom_call_target="tpu_custom_call" | custom-call | tf_op jit(solution)/shard_map/pick_relayed/pallas_call | solution.py:134
  62.0 1.8 pick_own.1
  66.1 3.5 %collective-permute-start.1 = (bf16[1,192,768]{2,1,0:T(8,128)(2,1)}, bf16[1,192,768]{2,1,0:T(8,128)(2,1)S(1)}, u32[]{:S(2)}, u32[]{:S(2)}) collective-permute-start(bf16[1,192,768]{2,1,0:T(8,128)(2,1)} %get-tuple-element.32), channel_id=1, source_target_pairs={{0,64},{8,72},{16,80},{24,88},{32,96},{40,104},{48,112},{56,120},{... | collective-permute-start | bytes 884744 | tf_op jit(solution)/shard_map/ppermute | solution.py:26
  69.7 1.1 collective-permute-start.18
  70.7 2.6 collective-permute-start.19
  73.5 14.6 %collective-permute-done.refs_1_ = bf16[1,192,768]{2,1,0:T(8,128)(2,1)S(1)} collective-permute-done((bf16[1,192,768]{2,1,0:T(8,128)(2,1)}, bf16[1,192,768]{2,1,0:T(8,128)(2,1)S(1)}, u32[]{:S(2)}, u32[]{:S(2)}) %collective-permute-start) | collective-permute-done | bytes 294944 | tf_op jit(solution)/shard_map/ppermute | solution.py:26
  88.8 2.8 collective-permute-done.1.refs_2_
  92.4 2.4 collective-permute-start.20
  95.6 2.0 collective-permute-start.16
  99.4 2.3 collective-permute-start.22
  104.7 7.2 %collective-permute-done.16.refs_6_ = bf16[3,192,768]{2,1,0:T(8,128)(2,1)S(1)} collective-permute-done((bf16[3,192,768]{2,1,0:T(8,128)(2,1)}, bf16[3,192,768]{2,1,0:T(8,128)(2,1)S(1)}, u32[]{:S(2)}, u32[]{:S(2)}) %collective-permute-start.16) | collective-permute-done | bytes 884768 | tf_op jit(solution)/shard_map/ppermute | solution.py:26
  111.8 20.7 %collective-permute-done.17.refs_7_ = bf16[3,192,768]{2,1,0:T(8,128)(2,1)} collective-permute-done((bf16[3,192,768]{2,1,0:T(8,128)(2,1)}, bf16[3,192,768]{2,1,0:T(8,128)(2,1)}, u32[]{:S(2)}, u32[]{:S(2)}) %collective-permute-start.17) | collective-permute-done | bytes 884768 | tf_op jit(solution)/shard_map/ppermute | solution.py:26
  132.6 2.7 collective-permute-done.23.refs_14_
  135.3 1.1 copy-done.2
  136.4 1.0 copy-done.5
  138.3 1.0 copy-done.11
  139.3 1.0 copy-done.13
  141.2 5.6 %pair_products.5 = (bf16[2,384,768]{2,1,0:T(8,128)(2,1)S(1)}, bf16[2,384,768]{2,1,0:T(8,128)(2,1)S(1)}) custom-call(s32[4]{0:T(128)S(1)} %get-tuple-element.80.left_ref, s32[4]{0:T(128)S(1)} %get-tuple-element.78.right_ref, bf16[384,768]{1,0:T(8,128)(2,1)S(1)} %copy-done.2, bf16[1,192,768]{2,1,0:T(8,128)(2,1)S(1)} %copy-done.5, ...), custom_call_target="tpu_custom_call" | custom-call | tf_op jit(solution)/shard_map/pair_products/pallas_call | solution.py:181
  146.8 3.7 %collective-permute-start.27 = (bf16[2,384,768]{2,1,0:T(8,128)(2,1)S(1)}, bf16[2,384,768]{2,1,0:T(8,128)(2,1)S(1)}, u32[]{:S(2)}, u32[]{:S(2)}) collective-permute-start(bf16[2,384,768]{2,1,0:T(8,128)(2,1)S(1)} %get-tuple-element.49), channel_id=1, source_target_pairs={{0,4},{1,5},{2,6},{3,7},{4,0},{5,1},{6,2},{7,3},{8,12},{9,13},{10,... | collective-permute-start | bytes 3538952 | tf_op jit(solution)/shard_map/ppermute | solution.py:35
  150.5 9.7 %collective-permute-start.28 = (bf16[2,384,768]{2,1,0:T(8,128)(2,1)S(1)}, bf16[2,384,768]{2,1,0:T(8,128)(2,1)S(1)}, u32[]{:S(2)}, u32[]{:S(2)}) collective-permute-start(bf16[2,384,768]{2,1,0:T(8,128)(2,1)S(1)} %get-tuple-element.50), channel_id=1, source_target_pairs={{0,5},{1,4},{2,7},{3,6},{4,1},{5,0},{6,3},{7,2},{8,13},{9,12},{10,... | collective-permute-start | bytes 3538952 | tf_op jit(solution)/shard_map/ppermute | solution.py:35
  160.4 8.5 %pair_products.4 = (bf16[2,384,768]{2,1,0:T(8,128)(2,1)}, bf16[2,384,768]{2,1,0:T(8,128)(2,1)}, bf16[2,384,768]{2,1,0:T(8,128)(2,1)}, bf16[2,384,768]{2,1,0:T(8,128)(2,1)}) custom-call(s32[8]{0:T(128)S(1)} %slice.51.left_ref, s32[8]{0:T(128)S(1)} %slice.52.right_ref, bf16[384,768]{1,0:T(8,128)(2,1)S(1)} %copy-done.2, bf16[1,192,768]{2,1,0:T(8,128)(2,1)S(1)} %copy-done.6, ...), custom_call_target="tpu_custom_call" | custom-call | tf_op jit(solution)/shard_map/pair_products/pallas_call | solution.py:181
  168.9 1.3 collective-permute-start.25
  170.2 2.7 collective-permute-start.29
  172.8 6.1 %pair_products.3 = (bf16[2,384,768]{2,1,0:T(8,128)(2,1)}, bf16[2,384,768]{2,1,0:T(8,128)(2,1)S(1)}) custom-call(s32[4]{0:T(128)S(1)} %get-tuple-element.81.left_ref, s32[4]{0:T(128)S(1)} %get-tuple-element.79.right_ref, bf16[384,768]{1,0:T(8,128)(2,1)S(1)} %copy-done.3, bf16[1,192,768]{2,1,0:T(8,128)(2,1)S(1)} %copy-done.6, ...), custom_call_target="tpu_custom_call" | custom-call | tf_op jit(solution)/shard_map/pair_products/pallas_call | solution.py:181
  179.0 1.0 copy-done.22
  180.0 1.0 copy-done.18
  181.0 10.7 %collective-permute-start.30 = (bf16[2,384,768]{2,1,0:T(8,128)(2,1)}, bf16[2,384,768]{2,1,0:T(8,128)(2,1)S(1)}, u32[]{:S(2)}, u32[]{:S(2)}) collective-permute-start(bf16[2,384,768]{2,1,0:T(8,128)(2,1)} %get-tuple-element.52), channel_id=1, source_target_pairs={{0,7},{1,6},{2,1},{3,0},{4,3},{5,2},{6,5},{7,4},{8,15},{9,14},{10,... | collective-permute-start | bytes 3538952 | tf_op jit(solution)/shard_map/ppermute | solution.py:35
  191.7 20.3 %collective-permute-done.28.refs_5_ = bf16[2,384,768]{2,1,0:T(8,128)(2,1)S(1)} collective-permute-done((bf16[2,384,768]{2,1,0:T(8,128)(2,1)S(1)}, bf16[2,384,768]{2,1,0:T(8,128)(2,1)S(1)}, u32[]{:S(2)}, u32[]{:S(2)}) %collective-permute-start.28) | collective-permute-done | bytes 1179680 | tf_op jit(solution)/shard_map/ppermute | solution.py:35
  212.0 1.0 copy-done.20
  213.4 1.3 dynamic_slice.6.live_ref
  216.9 10.8 %collective-permute-done.25.refs_2_ = bf16[2,384,768]{2,1,0:T(8,128)(2,1)} collective-permute-done((bf16[2,384,768]{2,1,0:T(8,128)(2,1)}, bf16[2,384,768]{2,1,0:T(8,128)(2,1)}, u32[]{:S(2)}, u32[]{:S(2)}) %collective-permute-start.25) | collective-permute-done | bytes 1179680 | tf_op jit(solution)/shard_map/ppermute | solution.py:35
  227.7 25.3 %collective-permute-done.26.refs_3_ = bf16[2,384,768]{2,1,0:T(8,128)(2,1)} collective-permute-done((bf16[2,384,768]{2,1,0:T(8,128)(2,1)}, bf16[2,384,768]{2,1,0:T(8,128)(2,1)}, u32[]{:S(2)}, u32[]{:S(2)}) %collective-permute-start.26) | collective-permute-done | bytes 1179680 | tf_op jit(solution)/shard_map/ppermute | solution.py:35
  253.4 1.3 copy-done.19
  254.6 1.3 copy-done.21
  255.9 1.3 copy-done.23
  257.2 10.4 %signed_sums.1 = (f32[4,384,768]{2,1,0:T(8,128)S(1)}, bf16[4,384,768]{2,1,0:T(8,128)(2,1)S(1)}) custom-call(s32[16]{0:T(128)S(1)} %get-tuple-element.64.left_ref, s32[16]{0:T(128)S(1)} %get-tuple-element.63.right_ref, s32[16]{0:T(128)S(1)} %fusion.12.target_ref, s32[16]{0:T(128)S(1)} %get-tuple-element.86.sign_ref, s32[1]{0:T(128)} %dynamic_slice.6.live_ref, ...), custom_call_target="tpu_custom_call" | custom-call | tf_op jit(solution)/shard_map/signed_sums/pallas_call | solution.py:238
  267.6 4.5 %collective-permute-done.31 = bf16[4,384,768]{2,1,0:T(8,128)(2,1)S(1)} collective-permute-done((bf16[4,384,768]{2,1,0:T(8,128)(2,1)S(1)}, bf16[4,384,768]{2,1,0:T(8,128)(2,1)S(1)}, u32[]{:S(2)}, u32[]{:S(2)}) %collective-permute-start.31) | collective-permute-done | bytes 2359328 | tf_op jit(solution)/shard_map/ppermute | solution.py:35
  272.9 3.7 %collective-permute-start.32 = (bf16[384,768]{1,0:T(8,128)(2,1)S(1)}, bf16[384,768]{1,0:T(8,128)(2,1)S(1)}, u32[]{:S(2)}, u32[]{:S(2)}) collective-permute-start(bf16[384,768]{1,0:T(8,128)(2,1)S(1)} %get-tuple-element.69), channel_id=1, source_target_pairs={{0,2},{1,3},{2,4},{3,5},{4,6},{5,7},{6,0},{7,1},{8,10},{9,11},{10,... | collective-permute-start | bytes 1769480 | tf_op jit(solution)/shard_map/ppermute | solution.py:35
  276.6 3.4 %collective-permute-start.33 = (bf16[384,768]{1,0:T(8,128)(2,1)S(1)}, bf16[384,768]{1,0:T(8,128)(2,1)S(1)}, u32[]{:S(2)}, u32[]{:S(2)}) collective-permute-start(bf16[384,768]{1,0:T(8,128)(2,1)S(1)} %get-tuple-element.71), channel_id=1, source_target_pairs={{0,4},{1,5},{2,6},{3,7},{4,0},{5,1},{6,2},{7,3},{8,12},{9,13},{10,... | collective-permute-start | bytes 1769480 | tf_op jit(solution)/shard_map/ppermute | solution.py:35
  280.0 12.1 %collective-permute-done.32 = bf16[384,768]{1,0:T(8,128)(2,1)S(1)} collective-permute-done((bf16[384,768]{1,0:T(8,128)(2,1)S(1)}, bf16[384,768]{1,0:T(8,128)(2,1)S(1)}, u32[]{:S(2)}, u32[]{:S(2)}) %collective-permute-start.32) | collective-permute-done | bytes 589856 | tf_op jit(solution)/shard_map/ppermute | solution.py:35
  292.1 13.5 %collective-permute-done.33 = bf16[384,768]{1,0:T(8,128)(2,1)S(1)} collective-permute-done((bf16[384,768]{1,0:T(8,128)(2,1)S(1)}, bf16[384,768]{1,0:T(8,128)(2,1)S(1)}, u32[]{:S(2)}, u32[]{:S(2)}) %collective-permute-start.33) | collective-permute-done | bytes 589856 | tf_op jit(solution)/shard_map/ppermute | solution.py:35
  305.7 1.3 fusion.3
  (145 shorter events, 26.2 us)
Async XLA Ops:
  0.0 39.1 %copy-start.44 = (s32[128,16]{0,1:T(8,128)S(1)}, s32[128,16]{0,1:T(8,128)}, u32[]{:S(2)}) copy-start(s32[128,16]{0,1:T(8,128)} %param.14) | copy-start | bytes 24580
  2.6 16.5 %collective-permute-start.9 = (bf16[2,192,768]{2,1,0:T(8,128)(2,1)S(1)}, bf16[2,192,768]{2,1,0:T(8,128)(2,1)S(1)}, u32[]{:S(2)}, u32[]{:S(2)}) collective-permute-start(bf16[2,192,768]{2,1,0:T(8,128)(2,1)S(1)} %get-tuple-element.75), channel_id=1, source_target_pairs={{0,32},{8,40},{16,48},{24,56},{32,64},{40,72},{48,80},{56,88},{64,... | collective-permute-start | bytes 1769480 | tf_op jit(solution)/shard_map/ppermute | solution.py:26
  4.7 15.7 %collective-permute-start.12 = (bf16[2,192,768]{2,1,0:T(8,128)(2,1)S(1)}, bf16[2,192,768]{2,1,0:T(8,128)(2,1)S(1)}, u32[]{:S(2)}, u32[]{:S(2)}) collective-permute-start(bf16[2,192,768]{2,1,0:T(8,128)(2,1)S(1)} %get-tuple-element.72), channel_id=1, source_target_pairs={{0,96},{8,104},{16,112},{24,120},{32,0},{40,8},{48,16},{56,24},{64... | collective-permute-start | bytes 1769480 | tf_op jit(solution)/shard_map/ppermute | solution.py:26
  6.1 15.4 %collective-permute-start.3 = (bf16[2,192,768]{2,1,0:T(8,128)(2,1)}, bf16[2,192,768]{2,1,0:T(8,128)(2,1)S(1)}, u32[]{:S(2)}, u32[]{:S(2)}) collective-permute-start(bf16[2,192,768]{2,1,0:T(8,128)(2,1)} %get-tuple-element.74), channel_id=1, source_target_pairs={{0,8},{8,16},{16,24},{24,0},{32,40},{40,48},{48,56},{56,32},{64,72... | collective-permute-start | bytes 1769480 | tf_op jit(solution)/shard_map/ppermute | solution.py:26
  7.3 15.7 %collective-permute-start.6 = (bf16[2,192,768]{2,1,0:T(8,128)(2,1)S(1)}, bf16[2,192,768]{2,1,0:T(8,128)(2,1)S(1)}, u32[]{:S(2)}, u32[]{:S(2)}) collective-permute-start(bf16[2,192,768]{2,1,0:T(8,128)(2,1)S(1)} %get-tuple-element.73), channel_id=1, source_target_pairs={{0,24},{8,0},{16,8},{24,16},{32,56},{40,32},{48,40},{56,48},{64,88... | collective-permute-start | bytes 1769480 | tf_op jit(solution)/shard_map/ppermute | solution.py:26
  8.8 22.9 %collective-permute-start.10 = (bf16[2,192,768]{2,1,0:T(8,128)(2,1)S(1)}, bf16[2,192,768]{2,1,0:T(8,128)(2,1)S(1)}, u32[]{:S(2)}, u32[]{:S(2)}) collective-permute-start(bf16[2,192,768]{2,1,0:T(8,128)(2,1)S(1)} %get-tuple-element.72), channel_id=1, source_target_pairs={{0,32},{8,40},{16,48},{24,56},{32,64},{40,72},{48,80},{56,88},{64,... | collective-permute-start | bytes 1769480 | tf_op jit(solution)/shard_map/ppermute | solution.py:26
  19.1 14.8 %collective-permute-start.14 = (bf16[2,192,768]{2,1,0:T(8,128)(2,1)S(1)}, bf16[2,192,768]{2,1,0:T(8,128)(2,1)S(1)}, u32[]{:S(2)}, u32[]{:S(2)}) collective-permute-start(bf16[2,192,768]{2,1,0:T(8,128)(2,1)S(1)} %get-tuple-element.75), channel_id=1, source_target_pairs={{0,96},{8,104},{16,112},{24,120},{32,0},{40,8},{48,16},{56,24},{64... | collective-permute-start | bytes 1769480 | tf_op jit(solution)/shard_map/ppermute | solution.py:26
  20.4 15.6 %collective-permute-start.4 = (bf16[2,192,768]{2,1,0:T(8,128)(2,1)S(1)}, bf16[2,192,768]{2,1,0:T(8,128)(2,1)S(1)}, u32[]{:S(2)}, u32[]{:S(2)}) collective-permute-start(bf16[2,192,768]{2,1,0:T(8,128)(2,1)S(1)} %get-tuple-element.73), channel_id=1, source_target_pairs={{0,8},{8,16},{16,24},{24,0},{32,40},{40,48},{48,56},{56,32},{64,72... | collective-permute-start | bytes 1769480 | tf_op jit(solution)/shard_map/ppermute | solution.py:26
  21.6 20.8 %collective-permute-start.8 = (bf16[2,192,768]{2,1,0:T(8,128)(2,1)}, bf16[2,192,768]{2,1,0:T(8,128)(2,1)}, u32[]{:S(2)}, u32[]{:S(2)}) collective-permute-start(bf16[2,192,768]{2,1,0:T(8,128)(2,1)} %get-tuple-element.74), channel_id=1, source_target_pairs={{0,24},{8,0},{16,8},{24,16},{32,56},{40,32},{48,40},{56,48},{64,88... | collective-permute-start | bytes 1769480 | tf_op jit(solution)/shard_map/ppermute | solution.py:26
  23.0 21.4 %collective-permute-start.11 = (bf16[2,192,768]{2,1,0:T(8,128)(2,1)S(1)}, bf16[2,192,768]{2,1,0:T(8,128)(2,1)}, u32[]{:S(2)}, u32[]{:S(2)}) collective-permute-start(bf16[2,192,768]{2,1,0:T(8,128)(2,1)S(1)} %collective-permute-done.9.refs_6_), channel_id=1, source_target_pairs={{0,32},{8,40},{16,48},{24,56},{32,64},{40,72},{48,80},{56,88},{64,... | collective-permute-start | bytes 1769480 | tf_op jit(solution)/shard_map/ppermute | solution.py:26
  32.5 12.7 %collective-permute-start.13 = (bf16[2,192,768]{2,1,0:T(8,128)(2,1)S(1)}, bf16[2,192,768]{2,1,0:T(8,128)(2,1)S(1)}, u32[]{:S(2)}, u32[]{:S(2)}) collective-permute-start(bf16[2,192,768]{2,1,0:T(8,128)(2,1)S(1)} %collective-permute-done.12.refs_11_), channel_id=1, source_target_pairs={{0,96},{8,104},{16,112},{24,120},{32,0},{40,8},{48,16},{56,24},{64... | collective-permute-start | bytes 1769480 | tf_op jit(solution)/shard_map/ppermute | solution.py:26
  34.7 13.3 %collective-permute-start.5 = (bf16[2,192,768]{2,1,0:T(8,128)(2,1)S(1)}, bf16[2,192,768]{2,1,0:T(8,128)(2,1)S(1)}, u32[]{:S(2)}, u32[]{:S(2)}) collective-permute-start(bf16[2,192,768]{2,1,0:T(8,128)(2,1)S(1)} %collective-permute-done.3.refs_0_), channel_id=1, source_target_pairs={{0,8},{8,16},{16,24},{24,0},{32,40},{40,48},{48,56},{56,32},{64,72... | collective-permute-start | bytes 1769480 | tf_op jit(solution)/shard_map/ppermute | solution.py:26
  36.8 12.0 %collective-permute-start.7 = (bf16[2,192,768]{2,1,0:T(8,128)(2,1)S(1)}, bf16[2,192,768]{2,1,0:T(8,128)(2,1)}, u32[]{:S(2)}, u32[]{:S(2)}) collective-permute-start(bf16[2,192,768]{2,1,0:T(8,128)(2,1)S(1)} %collective-permute-done.6.refs_5_), channel_id=1, source_target_pairs={{0,24},{8,0},{16,8},{24,16},{32,56},{40,32},{48,40},{56,48},{64,88... | collective-permute-start | bytes 1769480 | tf_op jit(solution)/shard_map/ppermute | solution.py:26
  48.8 1.1 copy-start.25
  49.9 1.1 copy-start.27
  50.9 1.1 copy-start.29
  52.0 1.1 copy-start.31
  53.1 1.1 copy-start.33
  54.1 1.1 copy-start.35
  55.2 6.8 %copy-start = (bf16[4,384,768]{2,1,0:T(8,128)(2,1)S(1)}, bf16[4,384,768]{2,1,0:T(8,128)(2,1)}, u32[]{:S(2)}) copy-start(bf16[4,384,768]{2,1,0:T(8,128)(2,1)} %nodes_ref.1) | copy-start | bytes 7077892
  61.6 2.2 copy-start.36
  61.6 2.2 copy-start.37
  61.6 11.8 %copy-start.43 = (s32[128,16]{0,1:T(8,128)S(1)}, s32[128,16]{0,1:T(8,128)}, u32[]{:S(2)}) copy-start(s32[128,16]{0,1:T(8,128)} %param.17) | copy-start | bytes 24580
  61.6 33.1 %copy-start.46 = (s32[8]{0:T(128)S(1)}, s32[8]{0:T(128)}, u32[]{:S(2)}) copy-start(s32[8]{0:T(128)} %constant.221.clone) | copy-start | bytes 100
  61.6 33.1 %copy-start.47 = (s32[8]{0:T(128)S(1)}, s32[8]{0:T(128)}, u32[]{:S(2)}) copy-start(s32[8]{0:T(128)} %constant.222.clone) | copy-start | bytes 100
  61.6 40.1 %collective-permute-start.15 = (bf16[3,192,768]{2,1,0:T(8,128)(2,1)}, bf16[3,192,768]{2,1,0:T(8,128)(2,1)S(1)}, u32[]{:S(2)}, u32[]{:S(2)}) collective-permute-start(bf16[3,192,768]{2,1,0:T(8,128)(2,1)} %get-tuple-element.35), channel_id=1, source_target_pairs={{0,32},{8,40},{16,48},{24,56},{32,64},{40,72},{48,80},{56,88},{64,... | collective-permute-start | bytes 2654216 | tf_op jit(solution)/shard_map/ppermute | solution.py:26
  66.1 22.0 %collective-permute-start = (bf16[1,192,768]{2,1,0:T(8,128)(2,1)}, bf16[1,192,768]{2,1,0:T(8,128)(2,1)S(1)}, u32[]{:S(2)}, u32[]{:S(2)}) collective-permute-start(bf16[1,192,768]{2,1,0:T(8,128)(2,1)} %get-tuple-element.31), channel_id=1, source_target_pairs={{0,32},{8,40},{16,48},{24,56},{32,64},{40,72},{48,80},{56,88},{64,... | collective-permute-start | bytes 884744 | tf_op jit(solution)/shard_map/ppermute | solution.py:26
  66.1 25.5 %collective-permute-start.1 = (bf16[1,192,768]{2,1,0:T(8,128)(2,1)}, bf16[1,192,768]{2,1,0:T(8,128)(2,1)S(1)}, u32[]{:S(2)}, u32[]{:S(2)}) collective-permute-start(bf16[1,192,768]{2,1,0:T(8,128)(2,1)} %get-tuple-element.32), channel_id=1, source_target_pairs={{0,64},{8,72},{16,80},{24,88},{32,96},{40,104},{48,112},{56,120},{... | collective-permute-start | bytes 884744 | tf_op jit(solution)/shard_map/ppermute | solution.py:26
  69.7 25.3 %collective-permute-start.18 = (bf16[1,192,768]{2,1,0:T(8,128)(2,1)}, bf16[1,192,768]{2,1,0:T(8,128)(2,1)S(1)}, u32[]{:S(2)}, u32[]{:S(2)}) collective-permute-start(bf16[1,192,768]{2,1,0:T(8,128)(2,1)} %get-tuple-element.38), channel_id=1, source_target_pairs={{0,8},{8,16},{16,24},{24,0},{32,40},{40,48},{48,56},{56,32},{64,72... | collective-permute-start | bytes 884744 | tf_op jit(solution)/shard_map/ppermute | solution.py:26
  70.7 27.0 %collective-permute-start.19 = (bf16[1,192,768]{2,1,0:T(8,128)(2,1)}, bf16[1,192,768]{2,1,0:T(8,128)(2,1)}, u32[]{:S(2)}, u32[]{:S(2)}) collective-permute-start(bf16[1,192,768]{2,1,0:T(8,128)(2,1)} %get-tuple-element.39), channel_id=1, source_target_pairs={{0,16},{8,24},{16,0},{24,8},{32,48},{40,56},{48,32},{56,40},{64,80... | collective-permute-start | bytes 884744 | tf_op jit(solution)/shard_map/ppermute | solution.py:26
  88.8 8.9 %collective-permute-start.2 = (bf16[1,192,768]{2,1,0:T(8,128)(2,1)}, bf16[1,192,768]{2,1,0:T(8,128)(2,1)S(1)}, u32[]{:S(2)}, u32[]{:S(2)}) collective-permute-start(bf16[1,192,768]{2,1,0:T(8,128)(2,1)} %copy-done.42), channel_id=1, source_target_pairs={{0,96},{8,104},{16,112},{24,120},{32,0},{40,8},{48,16},{56,24},{64... | collective-permute-start | bytes 884744 | tf_op jit(solution)/shard_map/ppermute | solution.py:26
  92.4 6.4 %collective-permute-start.20 = (bf16[1,192,768]{2,1,0:T(8,128)(2,1)}, bf16[1,192,768]{2,1,0:T(8,128)(2,1)S(1)}, u32[]{:S(2)}, u32[]{:S(2)}) collective-permute-start(bf16[1,192,768]{2,1,0:T(8,128)(2,1)} %copy-done.41), channel_id=1, source_target_pairs={{0,24},{8,0},{16,8},{24,16},{32,56},{40,32},{48,40},{56,48},{64,88... | collective-permute-start | bytes 884744 | tf_op jit(solution)/shard_map/ppermute | solution.py:26
  95.6 16.2 %collective-permute-start.16 = (bf16[3,192,768]{2,1,0:T(8,128)(2,1)}, bf16[3,192,768]{2,1,0:T(8,128)(2,1)S(1)}, u32[]{:S(2)}, u32[]{:S(2)}) collective-permute-start(bf16[3,192,768]{2,1,0:T(8,128)(2,1)} %copy-done.40), channel_id=1, source_target_pairs={{0,64},{8,72},{16,80},{24,88},{32,96},{40,104},{48,112},{56,120},{... | collective-permute-start | bytes 2654216 | tf_op jit(solution)/shard_map/ppermute | solution.py:26
  97.7 34.9 %collective-permute-start.17 = (bf16[3,192,768]{2,1,0:T(8,128)(2,1)}, bf16[3,192,768]{2,1,0:T(8,128)(2,1)}, u32[]{:S(2)}, u32[]{:S(2)}) collective-permute-start(bf16[3,192,768]{2,1,0:T(8,128)(2,1)} %copy-done.39), channel_id=1, source_target_pairs={{0,96},{8,104},{16,112},{24,120},{32,0},{40,8},{48,16},{56,24},{64... | collective-permute-start | bytes 2654216 | tf_op jit(solution)/shard_map/ppermute | solution.py:26
  98.4 34.2 %collective-permute-start.21 = (bf16[3,192,768]{2,1,0:T(8,128)(2,1)}, bf16[3,192,768]{2,1,0:T(8,128)(2,1)}, u32[]{:S(2)}, u32[]{:S(2)}) collective-permute-start(bf16[3,192,768]{2,1,0:T(8,128)(2,1)} %copy-done.38), channel_id=1, source_target_pairs={{0,8},{8,16},{16,24},{24,0},{32,40},{40,48},{48,56},{56,32},{64,72... | collective-permute-start | bytes 2654216 | tf_op jit(solution)/shard_map/ppermute | solution.py:26
  99.4 33.2 %collective-permute-start.22 = (bf16[3,192,768]{2,1,0:T(8,128)(2,1)}, bf16[3,192,768]{2,1,0:T(8,128)(2,1)}, u32[]{:S(2)}, u32[]{:S(2)}) collective-permute-start(bf16[3,192,768]{2,1,0:T(8,128)(2,1)} %copy-done.37), channel_id=1, source_target_pairs={{0,16},{8,24},{16,0},{24,8},{32,48},{40,56},{48,32},{56,40},{64,80... | collective-permute-start | bytes 2654216 | tf_op jit(solution)/shard_map/ppermute | solution.py:26
  101.7 33.6 %collective-permute-start.23 = (bf16[3,192,768]{2,1,0:T(8,128)(2,1)}, bf16[3,192,768]{2,1,0:T(8,128)(2,1)}, u32[]{:S(2)}, u32[]{:S(2)}) collective-permute-start(bf16[3,192,768]{2,1,0:T(8,128)(2,1)} %copy-done.36), channel_id=1, source_target_pairs={{0,24},{8,0},{16,8},{24,16},{32,56},{40,32},{48,40},{56,48},{64,88... | collective-permute-start | bytes 2654216 | tf_op jit(solution)/shard_map/ppermute | solution.py:26
  135.3 1.1 copy-start.2
  136.4 1.0 copy-start.5
  137.4 1.0 copy-start.8
  138.3 1.0 copy-start.11
  141.2 19.2 %copy-start.6 = (bf16[1,192,768]{2,1,0:T(8,128)(2,1)S(1)}, bf16[1,192,768]{2,1,0:T(8,128)(2,1)}, u32[]{:S(2)}) copy-start(bf16[1,192,768]{2,1,0:T(8,128)(2,1)} %copy-done.4) | copy-start | bytes 884740
  141.2 19.2 %copy-start.9 = (bf16[1,192,768]{2,1,0:T(8,128)(2,1)S(1)}, bf16[1,192,768]{2,1,0:T(8,128)(2,1)}, u32[]{:S(2)}) copy-start(bf16[1,192,768]{2,1,0:T(8,128)(2,1)} %copy-done.7) | copy-start | bytes 884740
  146.8 33.2 %collective-permute-start.27 = (bf16[2,384,768]{2,1,0:T(8,128)(2,1)S(1)}, bf16[2,384,768]{2,1,0:T(8,128)(2,1)S(1)}, u32[]{:S(2)}, u32[]{:S(2)}) collective-permute-start(bf16[2,384,768]{2,1,0:T(8,128)(2,1)S(1)} %get-tuple-element.49), channel_id=1, source_target_pairs={{0,4},{1,5},{2,6},{3,7},{4,0},{5,1},{6,2},{7,3},{8,12},{9,13},{10,... | collective-permute-start | bytes 3538952 | tf_op jit(solution)/shard_map/ppermute | solution.py:35
  150.5 61.5 %collective-permute-start.28 = (bf16[2,384,768]{2,1,0:T(8,128)(2,1)S(1)}, bf16[2,384,768]{2,1,0:T(8,128)(2,1)S(1)}, u32[]{:S(2)}, u32[]{:S(2)}) collective-permute-start(bf16[2,384,768]{2,1,0:T(8,128)(2,1)S(1)} %get-tuple-element.50), channel_id=1, source_target_pairs={{0,5},{1,4},{2,7},{3,6},{4,1},{5,0},{6,3},{7,2},{8,13},{9,12},{10,... | collective-permute-start | bytes 3538952 | tf_op jit(solution)/shard_map/ppermute | solution.py:35
  160.4 12.4 %copy-start.3 = (bf16[384,768]{1,0:T(8,128)(2,1)S(1)}, bf16[384,768]{1,0:T(8,128)(2,1)}, u32[]{:S(2)}) copy-start(bf16[384,768]{1,0:T(8,128)(2,1)} %copy-done.1) | copy-start | bytes 1769476
  160.4 12.4 %copy-start.14 = (bf16[1,192,768]{2,1,0:T(8,128)(2,1)S(1)}, bf16[1,192,768]{2,1,0:T(8,128)(2,1)}, u32[]{:S(2)}) copy-start(bf16[1,192,768]{2,1,0:T(8,128)(2,1)} %copy-done.12) | copy-start | bytes 884740
  160.4 12.4 %copy-start.17 = (bf16[1,192,768]{2,1,0:T(8,128)(2,1)S(1)}, bf16[1,192,768]{2,1,0:T(8,128)(2,1)}, u32[]{:S(2)}) copy-start(bf16[1,192,768]{2,1,0:T(8,128)(2,1)} %copy-done.15) | copy-start | bytes 884740
  168.9 58.8 %collective-permute-start.25 = (bf16[2,384,768]{2,1,0:T(8,128)(2,1)}, bf16[2,384,768]{2,1,0:T(8,128)(2,1)}, u32[]{:S(2)}, u32[]{:S(2)}) collective-permute-start(bf16[2,384,768]{2,1,0:T(8,128)(2,1)} %get-tuple-element.47), channel_id=1, source_target_pairs={{0,2},{1,3},{2,4},{3,5},{4,6},{5,7},{6,0},{7,1},{8,10},{9,11},{10,... | collective-permute-start | bytes 3538952 | tf_op jit(solution)/shard_map/ppermute | solution.py:35
  170.2 82.8 %collective-permute-start.26 = (bf16[2,384,768]{2,1,0:T(8,128)(2,1)}, bf16[2,384,768]{2,1,0:T(8,128)(2,1)}, u32[]{:S(2)}, u32[]{:S(2)}) collective-permute-start(bf16[2,384,768]{2,1,0:T(8,128)(2,1)} %get-tuple-element.48), channel_id=1, source_target_pairs={{0,3},{1,2},{2,5},{3,4},{4,7},{5,6},{6,1},{7,0},{8,11},{9,10},{10,... | collective-permute-start | bytes 3538952 | tf_op jit(solution)/shard_map/ppermute | solution.py:35
  170.2 82.8 %collective-permute-start.29 = (bf16[2,384,768]{2,1,0:T(8,128)(2,1)}, bf16[2,384,768]{2,1,0:T(8,128)(2,1)}, u32[]{:S(2)}, u32[]{:S(2)}) collective-permute-start(bf16[2,384,768]{2,1,0:T(8,128)(2,1)} %get-tuple-element.51), channel_id=1, source_target_pairs={{0,6},{1,7},{2,0},{3,1},{4,2},{5,3},{6,4},{7,5},{8,14},{9,15},{10,... | collective-permute-start | bytes 3538952 | tf_op jit(solution)/shard_map/ppermute | solution.py:35
  172.8 41.8 %copy-start.45 = (s32[128,16]{0,1:T(8,128)S(1)}, s32[128,16]{0,1:T(8,128)}, u32[]{:S(2)}) copy-start(s32[128,16]{0,1:T(8,128)} %param.19) | copy-start | bytes 24580
  179.0 1.0 copy-start.22
  180.0 1.0 copy-start.18
  181.0 72.3 %collective-permute-start.30 = (bf16[2,384,768]{2,1,0:T(8,128)(2,1)}, bf16[2,384,768]{2,1,0:T(8,128)(2,1)S(1)}, u32[]{:S(2)}, u32[]{:S(2)}) collective-permute-start(bf16[2,384,768]{2,1,0:T(8,128)(2,1)} %get-tuple-element.52), channel_id=1, source_target_pairs={{0,7},{1,6},{2,1},{3,0},{4,3},{5,2},{6,5},{7,4},{8,15},{9,14},{10,... | collective-permute-start | bytes 3538952 | tf_op jit(solution)/shard_map/ppermute | solution.py:35
  212.0 1.0 copy-start.20
  213.0 40.4 %collective-permute-start.24 = (bf16[2,384,768]{2,1,0:T(8,128)(2,1)}, bf16[2,384,768]{2,1,0:T(8,128)(2,1)S(1)}, u32[]{:S(2)}, u32[]{:S(2)}) collective-permute-start(bf16[2,384,768]{2,1,0:T(8,128)(2,1)} %get-tuple-element.46), channel_id=1, source_target_pairs={{0,1},{1,0},{2,3},{3,2},{4,5},{5,4},{6,7},{7,6},{8,9},{9,8},{10,11... | collective-permute-start | bytes 3538952 | tf_op jit(solution)/shard_map/ppermute | solution.py:35
  253.4 1.3 copy-start.19
  254.6 1.3 copy-start.21
  255.9 1.3 copy-start.23
  267.5 4.6 %collective-permute-start.31 = (bf16[4,384,768]{2,1,0:T(8,128)(2,1)S(1)}, bf16[4,384,768]{2,1,0:T(8,128)(2,1)S(1)}, u32[]{:S(2)}, u32[]{:S(2)}) collective-permute-start(bf16[4,384,768]{2,1,0:T(8,128)(2,1)S(1)} %get-tuple-element.54), channel_id=1, source_target_pairs={{0,1},{1,0},{2,3},{3,2},{4,5},{5,4},{6,7},{7,6},{8,9},{9,8},{10,11... | collective-permute-start | bytes 7077896 | tf_op jit(solution)/shard_map/ppermute | solution.py:35
  272.9 19.2 %collective-permute-start.32 = (bf16[384,768]{1,0:T(8,128)(2,1)S(1)}, bf16[384,768]{1,0:T(8,128)(2,1)S(1)}, u32[]{:S(2)}, u32[]{:S(2)}) collective-permute-start(bf16[384,768]{1,0:T(8,128)(2,1)S(1)} %get-tuple-element.69), channel_id=1, source_target_pairs={{0,2},{1,3},{2,4},{3,5},{4,6},{5,7},{6,0},{7,1},{8,10},{9,11},{10,... | collective-permute-start | bytes 1769480 | tf_op jit(solution)/shard_map/ppermute | solution.py:35
  276.6 29.0 %collective-permute-start.33 = (bf16[384,768]{1,0:T(8,128)(2,1)S(1)}, bf16[384,768]{1,0:T(8,128)(2,1)S(1)}, u32[]{:S(2)}, u32[]{:S(2)}) collective-permute-start(bf16[384,768]{1,0:T(8,128)(2,1)S(1)} %get-tuple-element.71), channel_id=1, source_target_pairs={{0,4},{1,5},{2,6},{3,7},{4,0},{5,1},{6,2},{7,3},{8,12},{9,13},{10,... | collective-permute-start | bytes 1769480 | tf_op jit(solution)/shard_map/ppermute | solution.py:35
  280.0 25.7 %collective-permute-start.34 = (bf16[384,768]{1,0:T(8,128)(2,1)S(1)}, bf16[384,768]{1,0:T(8,128)(2,1)S(1)}, u32[]{:S(2)}, u32[]{:S(2)}) collective-permute-start(bf16[384,768]{1,0:T(8,128)(2,1)S(1)} %get-tuple-element.70), channel_id=1, source_target_pairs={{0,6},{1,7},{2,0},{3,1},{4,2},{5,3},{6,4},{7,5},{8,14},{9,15},{10,... | collective-permute-start | bytes 1769480 | tf_op jit(solution)/shard_map/ppermute | solution.py:35
  (19 other events, 15.5 us)
where the time goes:
time: 308 us; the launch traced here: 307 us
  waiting for transfers between devices  159 us (52%)
  starting transfers between devices  64.9 us (21%)
  local copies, waits for them, and re-layouts  40.6 us (13%)
  Pallas kernels  36 us (12%)
  other arithmetic  6.33 us (2%)
    ppermute x11, waiting for transfers between devices, shift_ops(): return lax.ppermute(value, 'ops', pairs)  86.9 us
    ppermute x24, waiting for transfers between devices, shift_tm(): return lax.ppermute(value, 'tm', pairs)  71.9 us
    ppermute x11, starting transfers between devices, shift_ops(): return lax.ppermute(value, 'ops', pairs)  35.4 us
    unnamed x98, local copies, waits for them, and re-layouts  33.5 us
    ppermute x24, starting transfers between devices, shift_tm(): return lax.ppermute(value, 'tm', pairs)  29.5 us
    pallas_call x3, Pallas kernels, pair_products(): pl.pallas_call(kernel, out_shape=[jax.ShapeDtypeStruct((2, rank, width),...  20.2 us
    pallas_call x1, Pallas kernels, signed_sums(): pl.pallas_call(kernel, out_shape=[jax.ShapeDtypeStruct((SIDE, rank, width...  10.4 us
  transfers between devices with their start and end apart: 35, of which 18 were waited for; matrix products, arithmetic and copies ran while one was open for 3% of the time, Pallas kernels for 5%

commit v1 on v0

v1 whole, which is shorter than its diff:
```python
import math

import jax
import jax.numpy as jnp
from jax import lax
from jax.experimental import pallas as pl
from jax.experimental.pallas import tpu as pltpu
from jax.sharding import PartitionSpec as P


ANY = pl.BlockSpec(memory_space=pl.ANY)
SMEM = pl.BlockSpec(memory_space=pltpu.SMEM)
SIDE = 4
OTHERS = (1, 2, 3)
FAR = ((2, 0), (2, 1))
NEAR = ((1, 0), (1, 1), (3, 0), (3, 1))
HERE = ((0, 1), (0, 0))

OWN, RELAY, LEFT, RIGHT, LEFT2, RIGHT2, TARGET, SIGN, LIVE = 0, 8, 32, 48, 64, 80, 96, 112, 128
PLAN_SIZE = 256


def shift_tm(value, dy, dx):
    pairs = [
        (y * SIDE + x, (y + dy) % SIDE * SIDE + (x + dx) % SIDE)
        for y in range(SIDE)
        for x in range(SIDE)
    ]
    return lax.ppermute(value, "tm", pairs)


def shift_ops(value, dz, dc):
    pairs = [
        (z * 2 + core, (z + dz) % SIDE * 2 + (core + dc) % 2)
        for z in range(SIDE)
        for core in range(2)
    ]
    return lax.ppermute(value, "ops", pairs)


def copy_all(copies):
    for copy in copies:
        copy.start()
    for copy in copies:
        copy.wait()


def make_plan(cap, first_pulls, first_left, first_right, second_pulls, second_left, second_right, live, ids, signs):
    reads = second_pulls.shape[1]

    def kernel(pulls, left, right, pulls2, left2, right2, live2, ids_ref, signs_ref, plan, slots, pairs, seen, place):
        time, group = lax.axis_index("tm"), lax.axis_index("ops")
        y, x, z, core = time >> 2, time & 3, group >> 1, group & 1
        worker = time * 8 + group

        readers = [(d, 0) for d in range(SIDE)] + [(0, d) for d in OTHERS]
        workers = [
            ((((y + dy) & 3) << 2) + ((x + dx) & 3)) * 8 + group for dy, dx in readers
        ]

        def invert(j, carry):
            for r, reader in enumerate(workers):
                pull = pulls[j, reader]
                slots[r, pull >> 5] = pull & 3
            return carry

        lax.fori_loop(0, pulls.shape[0], invert, 0)
        for n, d in enumerate(OTHERS):
            plan[OWN + n] = slots[d, time]
            plan[OWN + 3 + n] = slots[3 + d, time]
        plan[OWN + 6] = slots[0, time]
        for n, behind in enumerate(OTHERS):
            source_x = (y << 2) + ((x - behind) & 3)
            source_y = (((y - behind) & 3) << 2) + x
            for d in range(SIDE):
                plan[RELAY + d * 3 + n] = slots[d, source_x]
                plan[RELAY + (SIDE + d) * 3 + n] = slots[3 + d if d else 0, source_y]

        for n, (dz, dc) in enumerate(FAR + NEAR + HERE):
            reader = time * 8 + (((z + dz) & 3) << 1) + ((core + dc) & 1)

            def find(j, count, n=n, reader=reader):
                pair = pulls2[j, reader] - worker * cap
                here = jnp.logical_and(pair >= 0, pair < cap)

                @pl.when(here)
                def _():
                    pairs[2 * n + jnp.minimum(count, 1)] = pair

                return count + here.astype(jnp.int32)

            lax.fori_loop(0, reads, find, jnp.int32(0))

        def position(entry):
            source = pulls[entry, worker] >> 5
            return (((y - (source >> 2)) & 3) << 2) + ((x - (source & 3)) & 3)

        def products(n, carry):
            pair = pairs[n]
            plan[LEFT + n] = position(left[pair, worker])
            plan[RIGHT + n] = position(right[pair, worker])
            return carry

        lax.fori_loop(0, 16, products, 0)

        for g in range(8):
            seen[g] = 0

        def arrivals(j, carry):
            source = lax.div(pulls2[j, worker] - time * (8 * cap), jnp.int32(cap))
            offset = (((z - (source >> 1)) & 3) << 1) + ((core + source) & 1)
            earlier = seen[source]
            seen[source] = earlier + 1
            place[j] = offset * 2 + jnp.minimum(earlier, 1)
            return carry

        lax.fori_loop(0, reads, arrivals, 0)

        def terms(q, carry):
            plan[LEFT2 + q] = place[left2[q, worker]]
            plan[RIGHT2 + q] = place[right2[q, worker]]
            target = ids_ref[q, worker] - time * 8
            ahead = ((target >> 1) - z) & 3
            order = jnp.where(ahead == 2, 0, jnp.where(ahead == 1, 1, jnp.where(ahead == 3, 2, 3)))
            plan[TARGET + q] = order + ((target + core) & 1) * SIDE
            plan[SIGN + q] = signs_ref[q, worker]
            return carry

        lax.fori_loop(0, left2.shape[0], terms, 0)
        plan[LIVE] = live2[worker]

    return pl.pallas_call(
        kernel,
        out_shape=jax.ShapeDtypeStruct((PLAN_SIZE,), jnp.int32),
        in_specs=[SMEM] * 9,
        out_specs=SMEM,
        scratch_shapes=[
            pltpu.SMEM((8, 16), jnp.int32),
            pltpu.SMEM((16,), jnp.int32),
            pltpu.SMEM((8,), jnp.int32),
            pltpu.SMEM((16,), jnp.int32),
        ],
        compiler_params=pltpu.CompilerParams(vmem_limit_bytes=1 << 20),
        name="make_plan",
    )(first_pulls.T, first_left.T, first_right.T, second_pulls.T, second_left.T, second_right.T, live, ids.T, signs.T)


def stack_right(block, stacked, rank):
    stacked[:rank, :] = block
    stacked[rank:, :rank] = -block[:, rank:]
    stacked[rank:, rank:] = block[:, :rank]


def half_shape(nodes, count):
    return jax.ShapeDtypeStruct((count, nodes.shape[1] // 2, nodes.shape[2]), nodes.dtype)


def pick_own(plan, nodes):
    half = nodes.shape[1] // 2

    def kernel(plan_ref, nodes_ref, *refs):
        outs, sems = refs[:-1], refs[-1]
        copies = []
        for n in range(3):
            upper, lower = plan_ref[OWN + n], plan_ref[OWN + 3 + n]
            copies.append(
                pltpu.make_async_copy(nodes_ref.at[pl.ds(upper, 1), :half], outs[n], sems.at[n])
            )
            copies.append(
                pltpu.make_async_copy(
                    nodes_ref.at[pl.ds(lower, 1), half:], outs[3 + n], sems.at[3 + n]
                )
            )
        copies.append(
            pltpu.make_async_copy(nodes_ref.at[plan_ref[OWN + 6]], outs[6], sems.at[6])
        )
        copy_all(copies)

    return pl.pallas_call(
        kernel,
        out_shape=[half_shape(nodes, 1)] * 6
        + [jax.ShapeDtypeStruct(nodes.shape[1:], nodes.dtype)],
        in_specs=[SMEM, pl.BlockSpec(memory_space=pltpu.VMEM)],
        out_specs=[ANY] * 7,
        scratch_shapes=[pltpu.SemaphoreType.DMA((7,))],
        compiler_params=pltpu.CompilerParams(vmem_limit_bytes=6 << 20),
        name="pick_own",
    )(plan, nodes)


def pick_relayed(plan, across, along):
    def kernel(plan_ref, *refs):
        gathered, outs, sems = refs[:12], refs[12:20], refs[20]
        waits = []
        for line in range(2):
            for d in range(SIDE):
                for n in range(3):
                    slot = plan_ref[RELAY + (line * SIDE + d) * 3 + n]
                    low, high = gathered[(line * 3 + n) * 2], gathered[(line * 3 + n) * 2 + 1]
                    target = outs[line * SIDE + d].at[n]
                    sem = sems.at[(line * SIDE + d) * 3 + n]
                    inner = slot & 1

                    @pl.when(slot < 2)
                    def _(low=low, target=target, sem=sem, inner=inner):
                        pltpu.make_async_copy(low.at[inner], target, sem).start()

                    @pl.when(slot >= 2)
                    def _(high=high, target=target, sem=sem, inner=inner):
                        pltpu.make_async_copy(high.at[inner], target, sem).start()

                    waits.append(pltpu.make_async_copy(low.at[0], target, sem))
        for wait in waits:
            wait.wait()

    arrays = [array for pair in across + along for array in pair]
    shape = jax.ShapeDtypeStruct((3,) + arrays[0].shape[1:], arrays[0].dtype)
    outs = pl.pallas_call(
        kernel,
        out_shape=[shape] * 8,
        in_specs=[SMEM] + [pl.BlockSpec(memory_space=pltpu.VMEM)] * 12,
        out_specs=[ANY] * 8,
        scratch_shapes=[pltpu.SemaphoreType.DMA((24,))],
        compiler_params=pltpu.CompilerParams(vmem_limit_bytes=9 << 20),
        name="pick_relayed",
    )(plan, *arrays)
    return outs[:4], outs[4:]


def pair_products(plan, first, outputs, pieces, norm):
    own, upper, lower = pieces
    rank, width = own.shape
    half = rank // 2
    upper_line, upper_far, lower_line, lower_far = *upper, *lower

    def kernel(plan_ref, *refs):
        own_ref, rest = refs[0], refs[1:15]
        outs, (blocks, stacked, sems) = refs[15 : 15 + outputs], refs[15 + outputs :]
        step = pl.program_id(0)

        @pl.when(step == 0)
        def _():
            pairs = [(own_ref, blocks.at[0, 0])]
            for n, d in enumerate(OTHERS):
                pairs.append((rest[n], blocks.at[d, pl.ds(0, 1), :half]))
                pairs.append((rest[7 + n], blocks.at[pl.ds(0, 1), d, half:]))
            for d in range(SIDE):
                pairs.append((rest[3 + d], blocks.at[d, pl.ds(1, 3), :half]))
                pairs.append((rest[10 + d], blocks.at[pl.ds(1, 3), d, half:]))
            copy_all(
                [
                    pltpu.make_async_copy(source, target, sems.at[n])
                    for n, (source, target) in enumerate(pairs)
                ]
            )

        for n, out_ref in enumerate(outs):
            index = first + n * 2 + step
            a, b = plan_ref[LEFT + index], plan_ref[RIGHT + index]
            stack_right(blocks[b >> 2, b & 3], stacked, rank)
            product = jnp.dot(
                blocks[a >> 2, a & 3], stacked[...], preferred_element_type=jnp.float32
            )
            out_ref[...] = (product * norm).astype(out_ref.dtype)

    return pl.pallas_call(
        kernel,
        out_shape=[jax.ShapeDtypeStruct((2, rank, width), jnp.bfloat16)] * outputs,
        grid=(2,),
        in_specs=[SMEM] + [ANY] * 15,
        out_specs=[pl.BlockSpec((None, rank, width), lambda i: (i, 0, 0))] * outputs,
        scratch_shapes=[
            pltpu.VMEM((SIDE, SIDE, rank, width), jnp.bfloat16),
            pltpu.VMEM((width, width), jnp.bfloat16),
            pltpu.SemaphoreType.DMA((15,)),
        ],
        compiler_params=pltpu.CompilerParams(vmem_limit_bytes=20 << 20),
        name="pair_products",
    )(plan, own, *upper_line, *upper_far, *lower_line, *lower_far)


def signed_sums(plan, first, targets, pieces, norm):
    rank, width = pieces[0].shape[1:]
    count = len(pieces)

    def kernel(plan_ref, *refs):
        keep_ref, give_ref, blocks, stacked, sums, sems = refs[count:]
        copies = [
            pltpu.make_async_copy(refs[n], blocks.at[pl.ds(2 * n, 2)], sems.at[n])
            for n in range(count)
        ]
        for copy in copies:
            copy.start()
        keep_ref[...] = jnp.zeros_like(keep_ref)
        sums[...] = jnp.zeros_like(sums)
        for copy in copies:
            copy.wait()

        def pair(index, carry):
            code = plan_ref[TARGET + index]
            where = (code & 3) - first

            @pl.when(jnp.logical_and(where >= 0, where < targets))
            def _():
                stack_right(blocks[plan_ref[RIGHT2 + index]], stacked, rank)
                product = jnp.dot(
                    blocks[plan_ref[LEFT2 + index]],
                    stacked[...],
                    preferred_element_type=jnp.float32,
                )
                term = product * (plan_ref[SIGN + index].astype(jnp.float32) * norm)

                @pl.when(code < SIDE)
                def _():
                    keep_ref[where] += term

                @pl.when(code >= SIDE)
                def _():
                    sums[where] += term

            return carry

        lax.fori_loop(0, plan_ref[LIVE], pair, 0)
        give_ref[...] = sums[...].astype(give_ref.dtype)

    return pl.pallas_call(
        kernel,
        out_shape=[
            jax.ShapeDtypeStruct((targets, rank, width), jnp.float32),
            jax.ShapeDtypeStruct((targets, rank, width), jnp.bfloat16),
        ],
        in_specs=[SMEM] + [ANY] * count,
        out_specs=[pl.BlockSpec(memory_space=pltpu.VMEM)] * 2,
        scratch_shapes=[
            pltpu.VMEM((2 * count, rank, width), jnp.bfloat16),
            pltpu.VMEM((width, width), jnp.bfloat16),
            pltpu.VMEM((targets, rank, width), jnp.float32),
            pltpu.SemaphoreType.DMA((count,)),
        ],
        compiler_params=pltpu.CompilerParams(vmem_limit_bytes=28 << 20),
    )(plan, *pieces)


def gather_nodes(node_blocks, plan):
    half = node_blocks.shape[1] // 2
    upper = [node_blocks[:2, :half], node_blocks[2:, :half]]
    lower = [node_blocks[:2, half:], node_blocks[2:, half:]]
    up, down = {}, {}
    for part in range(2):
        up[1, part] = shift_tm(upper[part], 0, 1)
        down[1, part] = shift_tm(lower[part], 1, 0)
        up[3, 1 - part] = shift_tm(upper[1 - part], 0, 3)
        down[3, 1 - part] = shift_tm(lower[1 - part], 3, 0)
    up[2, 0] = shift_tm(up[1, 0], 0, 1)
    down[2, 0] = shift_tm(down[1, 0], 1, 0)
    up[2, 1] = shift_tm(up[3, 1], 0, 3)
    down[2, 1] = shift_tm(down[3, 1], 3, 0)
    picked = pick_own(plan, node_blocks)
    upper_line = [shift_tm(picked[n], d, 0) for n, d in enumerate(OTHERS)]
    lower_line = [shift_tm(picked[3 + n], 0, d) for n, d in enumerate(OTHERS)]
    along_y, along_x = pick_relayed(
        plan,
        [(up[d, 0], up[d, 1]) for d in OTHERS],
        [(down[d, 0], down[d, 1]) for d in OTHERS],
    )
    far_y, far_x = {0: along_y[0]}, {0: along_x[0]}
    for d in (2, 1, 3):
        far_y[d] = shift_tm(along_y[d], d, 0)
        far_x[d] = shift_tm(along_x[d], 0, d)
    upper_far = [far_y[d] for d in range(SIDE)]
    lower_far = [far_x[d] for d in range(SIDE)]
    return picked[6], (upper_line, upper_far), (lower_line, lower_far)


def body(
    node_blocks,
    first_pulls,
    first_left,
    first_right,
    first_live,
    second_pulls,
    second_left,
    second_right,
    second_live,
    diagram_ids,
    diagram_signs,
):
    norm = 1.0 / math.sqrt(2.0 * node_blocks.shape[1])
    plan = make_plan(
        first_left.shape[1],
        first_pulls,
        first_left,
        first_right,
        second_pulls,
        second_left,
        second_right,
        second_live,
        diagram_ids,
        diagram_signs,
    )
    pieces = gather_nodes(node_blocks, plan)
    arrived = {}
    done = 0
    for part in (FAR, NEAR, HERE):
        products = pair_products(plan, 2 * done, len(part), pieces, norm)
        for (dz, dc), product in zip(part, products):
            arrived[dz, dc] = product if (dz, dc) == (0, 0) else shift_ops(product, dz, dc)
        done += len(part)

    factors = [arrived[dz, dc] for dz in range(SIDE) for dc in range(2)]
    keep, give = signed_sums(plan, 0, 1, factors, norm)
    both = keep[0] + shift_ops(give[0], 0, 1).astype(jnp.float32)
    far = shift_ops(both.astype(jnp.bfloat16), 2, 0)
    keep, give = signed_sums(plan, 1, 3, factors, norm)
    both = keep + shift_ops(give, 0, 1).astype(jnp.float32)
    near = both.astype(jnp.bfloat16)
    total = both[2] + far.astype(jnp.float32)
    for n, dz in ((0, 1), (1, 3)):
        total = total + shift_ops(near[n], dz, 0).astype(jnp.float32)
    return total[None]


def solution(mesh):
    placed = (P(("tm", "ops"), None, None),) + (P(),) * 10
    return jax.shard_map(body, mesh=mesh, in_specs=placed, out_specs=P(("tm", "ops"), None, None), check_vma=False)
```

time: 308 us -> 279 us (0.906)
  local copies, waits for them, and re-layouts: 40.6 us -> 1.95 us
  starting transfers between devices: 64.9 us -> 82.4 us
  other arithmetic: 6.33 us -> 1.97 us
    unnamed x98 -> x20, local copies, waits for them, and re-layouts: 33.5 us -> 0.04 us
    ppermute x11 -> x12, starting transfers between devices: 35.4 us -> 52.9 us  [shift_ops(): return lax.ppermute(value, 'ops', pairs)]
    pallas_call x3, Pallas kernels: 20.2 us -> 13.9 us  [pair_products(): pl.pallas_call(kernel, out_shape=[jax.ShapeDtypeStruct((2, rank, width),...]
    pallas_call x2 -> x4, Pallas kernels: 14 us -> 20.1 us  [the longest x2 12.4 us: signed_sums(): pl.pallas_call(kernel, out_shape=[jax.ShapeDtypeStruct((targets, rank, wi...]
    ppermute x11 -> x12, waiting for transfers between devices: 86.9 us -> 84 us  [shift_ops(): return lax.ppermute(value, 'ops', pairs)]
  transfers between devices with their start and end apart: 35 -> 36, of which waited for: 18 -> 18; matrix products, arithmetic and copies ran while one was open for 3% -> 0% of each run, Pallas kernels for 5% -> 7%
where the time goes in v1:
time: 279 us; the launch traced here: 278 us
  waiting for transfers between devices  156 us (56%)
  starting transfers between devices  82.4 us (30%)
  Pallas kernels  35.1 us (13%)
    ppermute x12, waiting for transfers between devices, shift_ops(): return lax.ppermute(value, 'ops', pairs)  84 us
    ppermute x24, waiting for transfers between devices, shift_tm(): return lax.ppermute(value, 'tm', pairs)  71.8 us
    ppermute x12, starting transfers between devices, shift_ops(): return lax.ppermute(value, 'ops', pairs)  52.9 us
    ppermute x24, starting transfers between devices, shift_tm(): return lax.ppermute(value, 'tm', pairs)  29.4 us
    pallas_call x3, Pallas kernels, pair_products(): pl.pallas_call(kernel, out_shape=[jax.ShapeDtypeStruct((2, rank, width),...  13.9 us
    pallas_call x2, Pallas kernels, signed_sums(): pl.pallas_call(kernel, out_shape=[jax.ShapeDtypeStruct((targets, rank, wi...  12.4 us
  transfers between devices with their start and end apart: 36, of which 18 were waited for; matrix products, arithmetic and copies ran while one was open for 0% of the time, Pallas kernels for 7%

profile of v1, /device:TPU:1, one launch (start us, length us, event | category | flops | bytes accessed | tf_op | source)
XLA Modules:
  0.0 277.5 jit_solution(10318398381358513787)
XLA Ops:
  0.1 1.8 fusion.6
  1.9 2.2 collective-permute-start.9
  4.1 1.5 collective-permute-start.12
  5.6 1.2 collective-permute-start.3
  6.8 1.5 collective-permute-start.6
  8.3 0.0 collective-permute-start.10
  8.3 10.2 %collective-permute-done.9.refs_6_ = bf16[2,192,768]{2,1,0:T(8,128)(2,1)S(1)} collective-permute-done((bf16[2,192,768]{2,1,0:T(8,128)(2,1)S(1)}, bf16[2,192,768]{2,1,0:T(8,128)(2,1)S(1)}, u32[]{:S(2)}, u32[]{:S(2)}) %collective-permute-start.9) | collective-permute-done | bytes 589856 | tf_op jit(solution)/shard_map/ppermute | solution.py:29
  18.5 1.3 collective-permute-start.14
  19.7 0.0 collective-permute-done.12.refs_11_
  19.7 1.2 collective-permute-start.4
  21.0 1.5 collective-permute-start.8
  22.4 0.2 collective-permute-start.11
  22.6 8.5 %collective-permute-done.10.refs_7_ = bf16[2,192,768]{2,1,0:T(8,128)(2,1)S(1)} collective-permute-done((bf16[2,192,768]{2,1,0:T(8,128)(2,1)S(1)}, bf16[2,192,768]{2,1,0:T(8,128)(2,1)S(1)}, u32[]{:S(2)}, u32[]{:S(2)}) %collective-permute-start.10) | collective-permute-done | bytes 589856 | tf_op jit(solution)/shard_map/ppermute | solution.py:29
  31.1 1.3 collective-permute-start.13
  32.4 1.2 collective-permute-start.5
  33.6 1.5 collective-permute-start.7
  35.1 5.1 %make_plan.1.plan_ref = s32[256]{0:T(256)S(1)} custom-call(s32[16,128]{1,0:T(8,128)S(1)} %bitcast.31, s32[24,128]{1,0:T(8,128)S(1)} %bitcast.29, s32[24,128]{1,0:T(8,128)S(1)} %bitcast.30, s32[16,128]{1,0:T(8,128)S(1)} %bitcast.32, s32[16,128]{1,0:T(8,128)S(1)} %bitcast.33, s32[16,128]{1,0:T(8,128)S(1)} %bitcast.34, s32[128]{0:T(128)S(1)} %copy-done.9, ...), custom_call_target="tpu_custom_call" | custom-call | tf_op jit(solution)/shard_map/make_plan/pallas_call | solution.py:132
  40.3 3.5 %collective-permute-done.11.refs_8_ = bf16[2,192,768]{2,1,0:T(8,128)(2,1)S(1)} collective-permute-done((bf16[2,192,768]{2,1,0:T(8,128)(2,1)S(1)}, bf16[2,192,768]{2,1,0:T(8,128)(2,1)S(1)}, u32[]{:S(2)}, u32[]{:S(2)}) %collective-permute-start.11) | collective-permute-done | bytes 589856 | tf_op jit(solution)/shard_map/ppermute | solution.py:29
  43.7 1.8 collective-permute-done.5.refs_2_
  45.5 2.6 pick_relayed.1
  48.1 0.6 collective-permute-start.15
  48.7 1.1 pick_own.1
  49.9 0.7 collective-permute-start
  50.5 2.7 collective-permute-start.1
  53.3 0.9 collective-permute-start.18
  54.2 2.6 collective-permute-start.19
  56.8 16.9 %collective-permute-done.refs_1_ = bf16[1,192,768]{2,1,0:T(8,128)(2,1)S(1)} collective-permute-done((bf16[1,192,768]{2,1,0:T(8,128)(2,1)S(1)}, bf16[1,192,768]{2,1,0:T(8,128)(2,1)S(1)}, u32[]{:S(2)}, u32[]{:S(2)}) %collective-permute-start) | collective-permute-done | bytes 294944 | tf_op jit(solution)/shard_map/ppermute | solution.py:29
  73.7 4.9 %collective-permute-done.1.refs_2_ = bf16[1,192,768]{2,1,0:T(8,128)(2,1)S(1)} collective-permute-done((bf16[1,192,768]{2,1,0:T(8,128)(2,1)S(1)}, bf16[1,192,768]{2,1,0:T(8,128)(2,1)S(1)}, u32[]{:S(2)}, u32[]{:S(2)}) %collective-permute-start.1) | collective-permute-done | bytes 294944 | tf_op jit(solution)/shard_map/ppermute | solution.py:29
  78.6 2.2 collective-permute-start.20
  80.8 1.6 collective-permute-start.16
  82.5 0.1 collective-permute-start.21
  82.6 1.9 collective-permute-done.20.refs_10_
  84.5 1.9 collective-permute-start.22
  86.4 1.5 collective-permute-start.23
  87.9 6.3 %collective-permute-done.16.refs_6_ = bf16[3,192,768]{2,1,0:T(8,128)(2,1)S(1)} collective-permute-done((bf16[3,192,768]{2,1,0:T(8,128)(2,1)S(1)}, bf16[3,192,768]{2,1,0:T(8,128)(2,1)S(1)}, u32[]{:S(2)}, u32[]{:S(2)}) %collective-permute-start.16) | collective-permute-done | bytes 884768 | tf_op jit(solution)/shard_map/ppermute | solution.py:29
  94.2 16.4 %collective-permute-done.17.refs_7_ = bf16[3,192,768]{2,1,0:T(8,128)(2,1)S(1)} collective-permute-done((bf16[3,192,768]{2,1,0:T(8,128)(2,1)S(1)}, bf16[3,192,768]{2,1,0:T(8,128)(2,1)S(1)}, u32[]{:S(2)}, u32[]{:S(2)}) %collective-permute-start.17) | collective-permute-done | bytes 884768 | tf_op jit(solution)/shard_map/ppermute | solution.py:29
  110.6 1.5 collective-permute-done.23.refs_14_
  112.1 4.0 %pair_products.5 = (bf16[2,384,768]{2,1,0:T(8,128)(2,1)S(1)}, bf16[2,384,768]{2,1,0:T(8,128)(2,1)S(1)}) custom-call(s32[256]{0:T(256)S(1)} %make_plan.1.plan_ref, bf16[384,768]{1,0:T(8,128)(2,1)S(1)} %get-tuple-element.32.refs_0_, bf16[1,192,768]{2,1,0:T(8,128)(2,1)S(1)} %collective-permute-done.refs_1_, ...), custom_call_target="tpu_custom_call" | custom-call | tf_op jit(solution)/shard_map/pair_products/pallas_call | solution.py:266
  116.1 3.3 %collective-permute-start.27 = (bf16[2,384,768]{2,1,0:T(8,128)(2,1)S(1)}, bf16[2,384,768]{2,1,0:T(8,128)(2,1)S(1)}, u32[]{:S(2)}, u32[]{:S(2)}) collective-permute-start(bf16[2,384,768]{2,1,0:T(8,128)(2,1)S(1)} %get-tuple-element.51), channel_id=1, source_target_pairs={{0,4},{1,5},{2,6},{3,7},{4,0},{5,1},{6,2},{7,3},{8,12},{9,13},{10,... | collective-permute-start | bytes 3538952 | tf_op jit(solution)/shard_map/ppermute | solution.py:38
  119.5 19.1 %collective-permute-start.28 = (bf16[2,384,768]{2,1,0:T(8,128)(2,1)S(1)}, bf16[2,384,768]{2,1,0:T(8,128)(2,1)S(1)}, u32[]{:S(2)}, u32[]{:S(2)}) collective-permute-start(bf16[2,384,768]{2,1,0:T(8,128)(2,1)S(1)} %get-tuple-element.52), channel_id=1, source_target_pairs={{0,5},{1,4},{2,7},{3,6},{4,1},{5,0},{6,3},{7,2},{8,13},{9,12},{10,... | collective-permute-start | bytes 3538952 | tf_op jit(solution)/shard_map/ppermute | solution.py:38
  138.6 5.9 %pair_products.4 = (bf16[2,384,768]{2,1,0:T(8,128)(2,1)S(1)}, bf16[2,384,768]{2,1,0:T(8,128)(2,1)S(1)}, bf16[2,384,768]{2,1,0:T(8,128)(2,1)S(1)}, bf16[2,384,768]{2,1,0:T(8,128)(2,1)S(1)}) custom-call(s32[256]{0:T(256)S(1)} %make_plan.1.plan_ref, bf16[384,768]{1,0:T(8,128)(2,1)S(1)} %get-tuple-element.32.refs_0_, ...), custom_call_target="tpu_custom_call" | custom-call | tf_op jit(solution)/shard_map/pair_products/pallas_call | solution.py:266
  144.6 1.3 collective-permute-start.25
  145.8 2.7 collective-permute-start.29
  148.5 4.0 %pair_products.3 = (bf16[2,384,768]{2,1,0:T(8,128)(2,1)S(1)}, bf16[2,384,768]{2,1,0:T(8,128)(2,1)S(1)}) custom-call(s32[256]{0:T(256)S(1)} %make_plan.1.plan_ref, bf16[384,768]{1,0:T(8,128)(2,1)S(1)} %get-tuple-element.32.refs_0_, bf16[1,192,768]{2,1,0:T(8,128)(2,1)S(1)} %collective-permute-done.refs_1_, ...), custom_call_target="tpu_custom_call" | custom-call | tf_op jit(solution)/shard_map/pair_products/pallas_call | solution.py:266
  152.5 16.6 %collective-permute-start.30 = (bf16[2,384,768]{2,1,0:T(8,128)(2,1)S(1)}, bf16[2,384,768]{2,1,0:T(8,128)(2,1)S(1)}, u32[]{:S(2)}, u32[]{:S(2)}) collective-permute-start(bf16[2,384,768]{2,1,0:T(8,128)(2,1)S(1)} %get-tuple-element.54), channel_id=1, source_target_pairs={{0,7},{1,6},{2,1},{3,0},{4,3},{5,2},{6,5},{7,4},{8,15},{9,14},{10,... | collective-permute-start | bytes 3538952 | tf_op jit(solution)/shard_map/ppermute | solution.py:38
  169.1 18.3 %collective-permute-done.28.refs_5_ = bf16[2,384,768]{2,1,0:T(8,128)(2,1)S(1)} collective-permute-done((bf16[2,384,768]{2,1,0:T(8,128)(2,1)S(1)}, bf16[2,384,768]{2,1,0:T(8,128)(2,1)S(1)}, u32[]{:S(2)}, u32[]{:S(2)}) %collective-permute-start.28) | collective-permute-done | bytes 1179680 | tf_op jit(solution)/shard_map/ppermute | solution.py:38
  187.4 3.2 %collective-permute-start.24 = (bf16[2,384,768]{2,1,0:T(8,128)(2,1)S(1)}, bf16[2,384,768]{2,1,0:T(8,128)(2,1)S(1)}, u32[]{:S(2)}, u32[]{:S(2)}) collective-permute-start(bf16[2,384,768]{2,1,0:T(8,128)(2,1)S(1)} %get-tuple-element.48), channel_id=1, source_target_pairs={{0,1},{1,0},{2,3},{3,2},{4,5},{5,4},{6,7},{7,6},{8,9},{9,8},{10,11... | collective-permute-start | bytes 3538952 | tf_op jit(solution)/shard_map/ppermute | solution.py:38
  190.6 12.7 %collective-permute-done.25.refs_2_ = bf16[2,384,768]{2,1,0:T(8,128)(2,1)S(1)} collective-permute-done((bf16[2,384,768]{2,1,0:T(8,128)(2,1)S(1)}, bf16[2,384,768]{2,1,0:T(8,128)(2,1)S(1)}, u32[]{:S(2)}, u32[]{:S(2)}) %collective-permute-start.25) | collective-permute-done | bytes 1179680 | tf_op jit(solution)/shard_map/ppermute | solution.py:38
  203.3 25.3 %collective-permute-done.26.refs_3_ = bf16[2,384,768]{2,1,0:T(8,128)(2,1)S(1)} collective-permute-done((bf16[2,384,768]{2,1,0:T(8,128)(2,1)S(1)}, bf16[2,384,768]{2,1,0:T(8,128)(2,1)S(1)}, u32[]{:S(2)}, u32[]{:S(2)}) %collective-permute-start.26) | collective-permute-done | bytes 1179680 | tf_op jit(solution)/shard_map/ppermute | solution.py:38
  228.5 0.7 collective-permute-done.30.refs_7_
  229.3 8.7 %shard_map.100 = (f32[3,384,768]{2,1,0:T(8,128)S(1)}, bf16[3,384,768]{2,1,0:T(8,128)(2,1)S(1)}) custom-call(s32[256]{0:T(256)S(1)} %make_plan.1.plan_ref, bf16[2,384,768]{2,1,0:T(8,128)(2,1)S(1)} %get-tuple-element.47.refs_0_, bf16[2,384,768]{2,1,0:T(8,128)(2,1)S(1)} %collective-permute-done.24.refs_1_, ...), custom_call_target="tpu_custom_call" | custom-call | tf_op jit(solution)/shard_map/pallas_call | solution.py:326
  238.0 0.1 collective-permute-start.31
  238.1 3.6 %shard_map.101 = (f32[1,384,768]{2,1,0:T(8,128)S(1)}, bf16[1,384,768]{2,1,0:T(8,128)(2,1)S(1)}) custom-call(s32[256]{0:T(256)S(1)} %make_plan.1.plan_ref, bf16[2,384,768]{2,1,0:T(8,128)(2,1)S(1)} %get-tuple-element.47.refs_0_, bf16[2,384,768]{2,1,0:T(8,128)(2,1)S(1)} %collective-permute-done.24.refs_1_, ...), custom_call_target="tpu_custom_call" | custom-call | tf_op jit(solution)/shard_map/pallas_call | solution.py:326
  241.8 0.1 collective-permute-start.32
  241.9 2.0 collective-permute-done.32
  243.9 0.1 fusion.4
  244.0 2.2 collective-permute-start.33
  246.2 0.6 fusion.5
  246.8 0.1 slice_bitcast_fusion.2
  246.9 4.4 %collective-permute-start.34 = (bf16[384,768]{1,0:T(8,128)(2,1)S(1)}, bf16[384,768]{1,0:T(8,128)(2,1)S(1)}, u32[]{:S(2)}, u32[]{:S(2)}) collective-permute-start(bf16[384,768]{1,0:T(8,128)(2,1)S(1)} %get-tuple-element.65), channel_id=1, source_target_pairs={{0,2},{1,3},{2,4},{3,5},{4,6},{5,7},{6,0},{7,1},{8,10},{9,11},{10,... | collective-permute-start | bytes 1769480 | tf_op jit(solution)/shard_map/ppermute | solution.py:38
  251.3 9.1 %collective-permute-done.33 = bf16[384,768]{1,0:T(8,128)(2,1)S(1)} collective-permute-done((bf16[384,768]{1,0:T(8,128)(2,1)S(1)}, bf16[384,768]{1,0:T(8,128)(2,1)S(1)}, u32[]{:S(2)}, u32[]{:S(2)}) %collective-permute-start.33) | collective-permute-done | bytes 589856 | tf_op jit(solution)/shard_map/ppermute | solution.py:38
  260.4 13.1 %collective-permute-done.34 = bf16[384,768]{1,0:T(8,128)(2,1)S(1)} collective-permute-done((bf16[384,768]{1,0:T(8,128)(2,1)S(1)}, bf16[384,768]{1,0:T(8,128)(2,1)S(1)}, u32[]{:S(2)}, u32[]{:S(2)}) %collective-permute-start.34) | collective-permute-done | bytes 589856 | tf_op jit(solution)/shard_map/ppermute | solution.py:38
  273.5 2.8 collective-permute-done.35
  276.3 1.2 fusion.3
  (41 shorter events, 0.1 us)
Async XLA Ops:
  0.0 35.1 %copy-start.3 = (s32[128,16]{0,1:T(8,128)S(1)}, s32[128,16]{0,1:T(8,128)}, u32[]{:S(2)}) copy-start(s32[128,16]{0,1:T(8,128)} %param.12) | copy-start | bytes 24580
  0.0 35.1 %copy-start.1 = (s32[128,24]{0,1:T(8,128)S(1)}, s32[128,24]{0,1:T(8,128)}, u32[]{:S(2)}) copy-start(s32[128,24]{0,1:T(8,128)} %param.13) | copy-start | bytes 36868
  0.0 35.1 %copy-start.2 = (s32[128,24]{0,1:T(8,128)S(1)}, s32[128,24]{0,1:T(8,128)}, u32[]{:S(2)}) copy-start(s32[128,24]{0,1:T(8,128)} %param.14) | copy-start | bytes 36868
  0.0 35.1 %copy-start.4 = (s32[128,16]{0,1:T(8,128)S(1)}, s32[128,16]{0,1:T(8,128)}, u32[]{:S(2)}) copy-start(s32[128,16]{0,1:T(8,128)} %param.15) | copy-start | bytes 24580
  0.0 35.1 %copy-start.5 = (s32[128,16]{0,1:T(8,128)S(1)}, s32[128,16]{0,1:T(8,128)}, u32[]{:S(2)}) copy-start(s32[128,16]{0,1:T(8,128)} %param.16) | copy-start | bytes 24580
  0.0 35.1 %copy-start.6 = (s32[128,16]{0,1:T(8,128)S(1)}, s32[128,16]{0,1:T(8,128)}, u32[]{:S(2)}) copy-start(s32[128,16]{0,1:T(8,128)} %param.17) | copy-start | bytes 24580
  0.0 35.1 %copy-start.7 = (s32[128,16]{0,1:T(8,128)S(1)}, s32[128,16]{0,1:T(8,128)}, u32[]{:S(2)}) copy-start(s32[128,16]{0,1:T(8,128)} %param.19) | copy-start | bytes 24580
  0.0 35.1 %copy-start.8 = (s32[128,16]{0,1:T(8,128)S(1)}, s32[128,16]{0,1:T(8,128)}, u32[]{:S(2)}) copy-start(s32[128,16]{0,1:T(8,128)} %param.20) | copy-start | bytes 24580
  0.1 35.1 %copy-start.9 = (s32[128]{0:T(128)S(1)}, s32[128]{0:T(128)}, u32[]{:S(2)}) copy-start(s32[128]{0:T(128)} %live2.1) | copy-start | bytes 1540
  1.9 16.5 %collective-permute-start.9 = (bf16[2,192,768]{2,1,0:T(8,128)(2,1)S(1)}, bf16[2,192,768]{2,1,0:T(8,128)(2,1)S(1)}, u32[]{:S(2)}, u32[]{:S(2)}) collective-permute-start(bf16[2,192,768]{2,1,0:T(8,128)(2,1)S(1)} %get-tuple-element.64), channel_id=1, source_target_pairs={{0,32},{8,40},{16,48},{24,56},{32,64},{40,72},{48,80},{56,88},{64,... | collective-permute-start | bytes 1769480 | tf_op jit(solution)/shard_map/ppermute | solution.py:29
  4.1 15.7 %collective-permute-start.12 = (bf16[2,192,768]{2,1,0:T(8,128)(2,1)S(1)}, bf16[2,192,768]{2,1,0:T(8,128)(2,1)S(1)}, u32[]{:S(2)}, u32[]{:S(2)}) collective-permute-start(bf16[2,192,768]{2,1,0:T(8,128)(2,1)S(1)} %get-tuple-element.61), channel_id=1, source_target_pairs={{0,96},{8,104},{16,112},{24,120},{32,0},{40,8},{48,16},{56,24},{64... | collective-permute-start | bytes 1769480 | tf_op jit(solution)/shard_map/ppermute | solution.py:29
  5.6 15.3 %collective-permute-start.3 = (bf16[2,192,768]{2,1,0:T(8,128)(2,1)S(1)}, bf16[2,192,768]{2,1,0:T(8,128)(2,1)S(1)}, u32[]{:S(2)}, u32[]{:S(2)}) collective-permute-start(bf16[2,192,768]{2,1,0:T(8,128)(2,1)S(1)} %get-tuple-element.63), channel_id=1, source_target_pairs={{0,8},{8,16},{16,24},{24,0},{32,40},{40,48},{48,56},{56,32},{64,72... | collective-permute-start | bytes 1769480 | tf_op jit(solution)/shard_map/ppermute | solution.py:29
  6.8 15.6 %collective-permute-start.6 = (bf16[2,192,768]{2,1,0:T(8,128)(2,1)S(1)}, bf16[2,192,768]{2,1,0:T(8,128)(2,1)S(1)}, u32[]{:S(2)}, u32[]{:S(2)}) collective-permute-start(bf16[2,192,768]{2,1,0:T(8,128)(2,1)S(1)} %get-tuple-element.62), channel_id=1, source_target_pairs={{0,24},{8,0},{16,8},{24,16},{32,56},{40,32},{48,40},{56,48},{64,88... | collective-permute-start | bytes 1769480 | tf_op jit(solution)/shard_map/ppermute | solution.py:29
  8.3 22.8 %collective-permute-start.10 = (bf16[2,192,768]{2,1,0:T(8,128)(2,1)S(1)}, bf16[2,192,768]{2,1,0:T(8,128)(2,1)S(1)}, u32[]{:S(2)}, u32[]{:S(2)}) collective-permute-start(bf16[2,192,768]{2,1,0:T(8,128)(2,1)S(1)} %get-tuple-element.61), channel_id=1, source_target_pairs={{0,32},{8,40},{16,48},{24,56},{32,64},{40,72},{48,80},{56,88},{64,... | collective-permute-start | bytes 1769480 | tf_op jit(solution)/shard_map/ppermute | solution.py:29
  18.5 13.9 %collective-permute-start.14 = (bf16[2,192,768]{2,1,0:T(8,128)(2,1)S(1)}, bf16[2,192,768]{2,1,0:T(8,128)(2,1)S(1)}, u32[]{:S(2)}, u32[]{:S(2)}) collective-permute-start(bf16[2,192,768]{2,1,0:T(8,128)(2,1)S(1)} %get-tuple-element.64), channel_id=1, source_target_pairs={{0,96},{8,104},{16,112},{24,120},{32,0},{40,8},{48,16},{56,24},{64... | collective-permute-start | bytes 1769480 | tf_op jit(solution)/shard_map/ppermute | solution.py:29
  19.7 13.9 %collective-permute-start.4 = (bf16[2,192,768]{2,1,0:T(8,128)(2,1)S(1)}, bf16[2,192,768]{2,1,0:T(8,128)(2,1)S(1)}, u32[]{:S(2)}, u32[]{:S(2)}) collective-permute-start(bf16[2,192,768]{2,1,0:T(8,128)(2,1)S(1)} %get-tuple-element.62), channel_id=1, source_target_pairs={{0,8},{8,16},{16,24},{24,0},{32,40},{40,48},{48,56},{56,32},{64,72... | collective-permute-start | bytes 1769480 | tf_op jit(solution)/shard_map/ppermute | solution.py:29
  21.0 19.3 %collective-permute-start.8 = (bf16[2,192,768]{2,1,0:T(8,128)(2,1)S(1)}, bf16[2,192,768]{2,1,0:T(8,128)(2,1)S(1)}, u32[]{:S(2)}, u32[]{:S(2)}) collective-permute-start(bf16[2,192,768]{2,1,0:T(8,128)(2,1)S(1)} %get-tuple-element.63), channel_id=1, source_target_pairs={{0,24},{8,0},{16,8},{24,16},{32,56},{40,32},{48,40},{56,48},{64,88... | collective-permute-start | bytes 1769480 | tf_op jit(solution)/shard_map/ppermute | solution.py:29
  22.4 21.3 %collective-permute-start.11 = (bf16[2,192,768]{2,1,0:T(8,128)(2,1)S(1)}, bf16[2,192,768]{2,1,0:T(8,128)(2,1)S(1)}, u32[]{:S(2)}, u32[]{:S(2)}) collective-permute-start(bf16[2,192,768]{2,1,0:T(8,128)(2,1)S(1)} %collective-permute-done.9.refs_6_), channel_id=1, source_target_pairs={{0,32},{8,40},{16,48},{24,56},{32,64},{40,72},{48,80},{56,88},{64,... | collective-permute-start | bytes 1769480 | tf_op jit(solution)/shard_map/ppermute | solution.py:29
  31.1 12.6 %collective-permute-start.13 = (bf16[2,192,768]{2,1,0:T(8,128)(2,1)S(1)}, bf16[2,192,768]{2,1,0:T(8,128)(2,1)S(1)}, u32[]{:S(2)}, u32[]{:S(2)}) collective-permute-start(bf16[2,192,768]{2,1,0:T(8,128)(2,1)S(1)} %collective-permute-done.12.refs_11_), channel_id=1, source_target_pairs={{0,96},{8,104},{16,112},{24,120},{32,0},{40,8},{48,16},{56,24},{64... | collective-permute-start | bytes 1769480 | tf_op jit(solution)/shard_map/ppermute | solution.py:29
  32.4 13.2 %collective-permute-start.5 = (bf16[2,192,768]{2,1,0:T(8,128)(2,1)S(1)}, bf16[2,192,768]{2,1,0:T(8,128)(2,1)S(1)}, u32[]{:S(2)}, u32[]{:S(2)}) collective-permute-start(bf16[2,192,768]{2,1,0:T(8,128)(2,1)S(1)} %collective-permute-done.3.refs_0_), channel_id=1, source_target_pairs={{0,8},{8,16},{16,24},{24,0},{32,40},{40,48},{48,56},{56,32},{64,72... | collective-permute-start | bytes 1769480 | tf_op jit(solution)/shard_map/ppermute | solution.py:29
  33.6 11.9 %collective-permute-start.7 = (bf16[2,192,768]{2,1,0:T(8,128)(2,1)S(1)}, bf16[2,192,768]{2,1,0:T(8,128)(2,1)S(1)}, u32[]{:S(2)}, u32[]{:S(2)}) collective-permute-start(bf16[2,192,768]{2,1,0:T(8,128)(2,1)S(1)} %collective-permute-done.6.refs_5_), channel_id=1, source_target_pairs={{0,24},{8,0},{16,8},{24,16},{32,56},{40,32},{48,40},{56,48},{64,88... | collective-permute-start | bytes 1769480 | tf_op jit(solution)/shard_map/ppermute | solution.py:29
  45.5 3.2 %copy-start = (bf16[4,384,768]{2,1,0:T(8,128)(2,1)S(1)}, bf16[4,384,768]{2,1,0:T(8,128)(2,1)}, u32[]{:S(2)}) copy-start(bf16[4,384,768]{2,1,0:T(8,128)(2,1)} %nodes_ref.1) | copy-start | bytes 7077892
  48.1 38.3 %collective-permute-start.15 = (bf16[3,192,768]{2,1,0:T(8,128)(2,1)S(1)}, bf16[3,192,768]{2,1,0:T(8,128)(2,1)S(1)}, u32[]{:S(2)}, u32[]{:S(2)}) collective-permute-start(bf16[3,192,768]{2,1,0:T(8,128)(2,1)S(1)} %get-tuple-element.37), channel_id=1, source_target_pairs={{0,32},{8,40},{16,48},{24,56},{32,64},{40,72},{48,80},{56,88},{64,... | collective-permute-start | bytes 2654216 | tf_op jit(solution)/shard_map/ppermute | solution.py:29
  49.9 23.8 %collective-permute-start = (bf16[1,192,768]{2,1,0:T(8,128)(2,1)S(1)}, bf16[1,192,768]{2,1,0:T(8,128)(2,1)S(1)}, u32[]{:S(2)}, u32[]{:S(2)}) collective-permute-start(bf16[1,192,768]{2,1,0:T(8,128)(2,1)S(1)} %get-tuple-element.33), channel_id=1, source_target_pairs={{0,32},{8,40},{16,48},{24,56},{32,64},{40,72},{48,80},{56,88},{64,... | collective-permute-start | bytes 884744 | tf_op jit(solution)/shard_map/ppermute | solution.py:29
  50.5 28.1 %collective-permute-start.1 = (bf16[1,192,768]{2,1,0:T(8,128)(2,1)S(1)}, bf16[1,192,768]{2,1,0:T(8,128)(2,1)S(1)}, u32[]{:S(2)}, u32[]{:S(2)}) collective-permute-start(bf16[1,192,768]{2,1,0:T(8,128)(2,1)S(1)} %get-tuple-element.34), channel_id=1, source_target_pairs={{0,64},{8,72},{16,80},{24,88},{32,96},{40,104},{48,112},{56,120},{... | collective-permute-start | bytes 884744 | tf_op jit(solution)/shard_map/ppermute | solution.py:29
  53.3 27.6 %collective-permute-start.18 = (bf16[1,192,768]{2,1,0:T(8,128)(2,1)S(1)}, bf16[1,192,768]{2,1,0:T(8,128)(2,1)S(1)}, u32[]{:S(2)}, u32[]{:S(2)}) collective-permute-start(bf16[1,192,768]{2,1,0:T(8,128)(2,1)S(1)} %get-tuple-element.40), channel_id=1, source_target_pairs={{0,8},{8,16},{16,24},{24,0},{32,40},{40,48},{48,56},{56,32},{64,72... | collective-permute-start | bytes 884744 | tf_op jit(solution)/shard_map/ppermute | solution.py:29
  54.2 28.3 %collective-permute-start.19 = (bf16[1,192,768]{2,1,0:T(8,128)(2,1)S(1)}, bf16[1,192,768]{2,1,0:T(8,128)(2,1)S(1)}, u32[]{:S(2)}, u32[]{:S(2)}) collective-permute-start(bf16[1,192,768]{2,1,0:T(8,128)(2,1)S(1)} %get-tuple-element.41), channel_id=1, source_target_pairs={{0,16},{8,24},{16,0},{24,8},{32,48},{40,56},{48,32},{56,40},{64,80... | collective-permute-start | bytes 884744 | tf_op jit(solution)/shard_map/ppermute | solution.py:29
  73.7 8.8 %collective-permute-start.2 = (bf16[1,192,768]{2,1,0:T(8,128)(2,1)S(1)}, bf16[1,192,768]{2,1,0:T(8,128)(2,1)S(1)}, u32[]{:S(2)}, u32[]{:S(2)}) collective-permute-start(bf16[1,192,768]{2,1,0:T(8,128)(2,1)S(1)} %get-tuple-element.35), channel_id=1, source_target_pairs={{0,96},{8,104},{16,112},{24,120},{32,0},{40,8},{48,16},{56,24},{64... | collective-permute-start | bytes 884744 | tf_op jit(solution)/shard_map/ppermute | solution.py:29
  78.6 5.9 %collective-permute-start.20 = (bf16[1,192,768]{2,1,0:T(8,128)(2,1)S(1)}, bf16[1,192,768]{2,1,0:T(8,128)(2,1)S(1)}, u32[]{:S(2)}, u32[]{:S(2)}) collective-permute-start(bf16[1,192,768]{2,1,0:T(8,128)(2,1)S(1)} %get-tuple-element.42), channel_id=1, source_target_pairs={{0,24},{8,0},{16,8},{24,16},{32,56},{40,32},{48,40},{56,48},{64,88... | collective-permute-start | bytes 884744 | tf_op jit(solution)/shard_map/ppermute | solution.py:29
  80.8 13.4 %collective-permute-start.16 = (bf16[3,192,768]{2,1,0:T(8,128)(2,1)S(1)}, bf16[3,192,768]{2,1,0:T(8,128)(2,1)S(1)}, u32[]{:S(2)}, u32[]{:S(2)}) collective-permute-start(bf16[3,192,768]{2,1,0:T(8,128)(2,1)S(1)} %get-tuple-element.38), channel_id=1, source_target_pairs={{0,64},{8,72},{16,80},{24,88},{32,96},{40,104},{48,112},{56,120},{... | collective-permute-start | bytes 2654216 | tf_op jit(solution)/shard_map/ppermute | solution.py:29
  82.5 28.2 %collective-permute-start.17 = (bf16[3,192,768]{2,1,0:T(8,128)(2,1)S(1)}, bf16[3,192,768]{2,1,0:T(8,128)(2,1)S(1)}, u32[]{:S(2)}, u32[]{:S(2)}) collective-permute-start(bf16[3,192,768]{2,1,0:T(8,128)(2,1)S(1)} %get-tuple-element.39), channel_id=1, source_target_pairs={{0,96},{8,104},{16,112},{24,120},{32,0},{40,8},{48,16},{56,24},{64... | collective-permute-start | bytes 2654216 | tf_op jit(solution)/shard_map/ppermute | solution.py:29
  82.5 28.2 %collective-permute-start.21 = (bf16[3,192,768]{2,1,0:T(8,128)(2,1)S(1)}, bf16[3,192,768]{2,1,0:T(8,128)(2,1)S(1)}, u32[]{:S(2)}, u32[]{:S(2)}) collective-permute-start(bf16[3,192,768]{2,1,0:T(8,128)(2,1)S(1)} %get-tuple-element.44), channel_id=1, source_target_pairs={{0,8},{8,16},{16,24},{24,0},{32,40},{40,48},{48,56},{56,32},{64,72... | collective-permute-start | bytes 2654216 | tf_op jit(solution)/shard_map/ppermute | solution.py:29
  84.5 26.1 %collective-permute-start.22 = (bf16[3,192,768]{2,1,0:T(8,128)(2,1)S(1)}, bf16[3,192,768]{2,1,0:T(8,128)(2,1)S(1)}, u32[]{:S(2)}, u32[]{:S(2)}) collective-permute-start(bf16[3,192,768]{2,1,0:T(8,128)(2,1)S(1)} %get-tuple-element.45), channel_id=1, source_target_pairs={{0,16},{8,24},{16,0},{24,8},{32,48},{40,56},{48,32},{56,40},{64,80... | collective-permute-start | bytes 2654216 | tf_op jit(solution)/shard_map/ppermute | solution.py:29
  86.4 25.7 %collective-permute-start.23 = (bf16[3,192,768]{2,1,0:T(8,128)(2,1)S(1)}, bf16[3,192,768]{2,1,0:T(8,128)(2,1)S(1)}, u32[]{:S(2)}, u32[]{:S(2)}) collective-permute-start(bf16[3,192,768]{2,1,0:T(8,128)(2,1)S(1)} %get-tuple-element.46), channel_id=1, source_target_pairs={{0,24},{8,0},{16,8},{24,16},{32,56},{40,32},{48,40},{56,48},{64,88... | collective-permute-start | bytes 2654216 | tf_op jit(solution)/shard_map/ppermute | solution.py:29
  116.1 36.4 %collective-permute-start.27 = (bf16[2,384,768]{2,1,0:T(8,128)(2,1)S(1)}, bf16[2,384,768]{2,1,0:T(8,128)(2,1)S(1)}, u32[]{:S(2)}, u32[]{:S(2)}) collective-permute-start(bf16[2,384,768]{2,1,0:T(8,128)(2,1)S(1)} %get-tuple-element.51), channel_id=1, source_target_pairs={{0,4},{1,5},{2,6},{3,7},{4,0},{5,1},{6,2},{7,3},{8,12},{9,13},{10,... | collective-permute-start | bytes 3538952 | tf_op jit(solution)/shard_map/ppermute | solution.py:38
  119.5 67.9 %collective-permute-start.28 = (bf16[2,384,768]{2,1,0:T(8,128)(2,1)S(1)}, bf16[2,384,768]{2,1,0:T(8,128)(2,1)S(1)}, u32[]{:S(2)}, u32[]{:S(2)}) collective-permute-start(bf16[2,384,768]{2,1,0:T(8,128)(2,1)S(1)} %get-tuple-element.52), channel_id=1, source_target_pairs={{0,5},{1,4},{2,7},{3,6},{4,1},{5,0},{6,3},{7,2},{8,13},{9,12},{10,... | collective-permute-start | bytes 3538952 | tf_op jit(solution)/shard_map/ppermute | solution.py:38
  144.6 58.7 %collective-permute-start.25 = (bf16[2,384,768]{2,1,0:T(8,128)(2,1)S(1)}, bf16[2,384,768]{2,1,0:T(8,128)(2,1)S(1)}, u32[]{:S(2)}, u32[]{:S(2)}) collective-permute-start(bf16[2,384,768]{2,1,0:T(8,128)(2,1)S(1)} %get-tuple-element.49), channel_id=1, source_target_pairs={{0,2},{1,3},{2,4},{3,5},{4,6},{5,7},{6,0},{7,1},{8,10},{9,11},{10,... | collective-permute-start | bytes 3538952 | tf_op jit(solution)/shard_map/ppermute | solution.py:38
  145.8 82.7 %collective-permute-start.26 = (bf16[2,384,768]{2,1,0:T(8,128)(2,1)S(1)}, bf16[2,384,768]{2,1,0:T(8,128)(2,1)S(1)}, u32[]{:S(2)}, u32[]{:S(2)}) collective-permute-start(bf16[2,384,768]{2,1,0:T(8,128)(2,1)S(1)} %get-tuple-element.50), channel_id=1, source_target_pairs={{0,3},{1,2},{2,5},{3,4},{4,7},{5,6},{6,1},{7,0},{8,11},{9,10},{10,... | collective-permute-start | bytes 3538952 | tf_op jit(solution)/shard_map/ppermute | solution.py:38
  145.8 82.7 %collective-permute-start.29 = (bf16[2,384,768]{2,1,0:T(8,128)(2,1)S(1)}, bf16[2,384,768]{2,1,0:T(8,128)(2,1)S(1)}, u32[]{:S(2)}, u32[]{:S(2)}) collective-permute-start(bf16[2,384,768]{2,1,0:T(8,128)(2,1)S(1)} %get-tuple-element.53), channel_id=1, source_target_pairs={{0,6},{1,7},{2,0},{3,1},{4,2},{5,3},{6,4},{7,5},{8,14},{9,15},{10,... | collective-permute-start | bytes 3538952 | tf_op jit(solution)/shard_map/ppermute | solution.py:38
  152.5 76.8 %collective-permute-start.30 = (bf16[2,384,768]{2,1,0:T(8,128)(2,1)S(1)}, bf16[2,384,768]{2,1,0:T(8,128)(2,1)S(1)}, u32[]{:S(2)}, u32[]{:S(2)}) collective-permute-start(bf16[2,384,768]{2,1,0:T(8,128)(2,1)S(1)} %get-tuple-element.54), channel_id=1, source_target_pairs={{0,7},{1,6},{2,1},{3,0},{4,3},{5,2},{6,5},{7,4},{8,15},{9,14},{10,... | collective-permute-start | bytes 3538952 | tf_op jit(solution)/shard_map/ppermute | solution.py:38
  187.4 41.9 %collective-permute-start.24 = (bf16[2,384,768]{2,1,0:T(8,128)(2,1)S(1)}, bf16[2,384,768]{2,1,0:T(8,128)(2,1)S(1)}, u32[]{:S(2)}, u32[]{:S(2)}) collective-permute-start(bf16[2,384,768]{2,1,0:T(8,128)(2,1)S(1)} %get-tuple-element.48), channel_id=1, source_target_pairs={{0,1},{1,0},{2,3},{3,2},{4,5},{5,4},{6,7},{7,6},{8,9},{9,8},{10,11... | collective-permute-start | bytes 3538952 | tf_op jit(solution)/shard_map/ppermute | solution.py:38
  238.0 8.2 %collective-permute-start.31 = (bf16[3,384,768]{2,1,0:T(8,128)(2,1)S(1)}, bf16[3,384,768]{2,1,0:T(8,128)(2,1)S(1)}, u32[]{:S(2)}, u32[]{:S(2)}) collective-permute-start(bf16[3,384,768]{2,1,0:T(8,128)(2,1)S(1)} %get-tuple-element.56), channel_id=1, source_target_pairs={{0,1},{1,0},{2,3},{3,2},{4,5},{5,4},{6,7},{7,6},{8,9},{9,8},{10,11... | collective-permute-start | bytes 5308424 | tf_op jit(solution)/shard_map/ppermute | solution.py:38
  241.8 2.1 collective-permute-start.32
  244.0 16.4 %collective-permute-start.33 = (bf16[384,768]{1,0:T(8,128)(2,1)S(1)}, bf16[384,768]{1,0:T(8,128)(2,1)S(1)}, u32[]{:S(2)}, u32[]{:S(2)}) collective-permute-start(bf16[384,768]{1,0:T(8,128)(2,1)S(1)} %fusion.4), channel_id=1, source_target_pairs={{0,4},{1,5},{2,6},{3,7},{4,0},{5,1},{6,2},{7,3},{8,12},{9,13},{10,... | collective-permute-start | bytes 1769480 | tf_op jit(solution)/shard_map/ppermute | solution.py:38
  246.9 26.6 %collective-permute-start.34 = (bf16[384,768]{1,0:T(8,128)(2,1)S(1)}, bf16[384,768]{1,0:T(8,128)(2,1)S(1)}, u32[]{:S(2)}, u32[]{:S(2)}) collective-permute-start(bf16[384,768]{1,0:T(8,128)(2,1)S(1)} %get-tuple-element.65), channel_id=1, source_target_pairs={{0,2},{1,3},{2,4},{3,5},{4,6},{5,7},{6,0},{7,1},{8,10},{9,11},{10,... | collective-permute-start | bytes 1769480 | tf_op jit(solution)/shard_map/ppermute | solution.py:38
  251.3 25.0 %collective-permute-start.35 = (bf16[384,768]{1,0:T(8,128)(2,1)S(1)}, bf16[384,768]{1,0:T(8,128)(2,1)S(1)}, u32[]{:S(2)}, u32[]{:S(2)}) collective-permute-start(bf16[384,768]{1,0:T(8,128)(2,1)S(1)} %get-tuple-element.66), channel_id=1, source_target_pairs={{0,6},{1,7},{2,0},{3,1},{4,2},{5,3},{6,4},{7,5},{8,14},{9,15},{10,... | collective-permute-start | bytes 1769480 | tf_op jit(solution)/shard_map/ppermute | solution.py:38

commit v2 on v1

--- a/solution.py
+++ b/solution.py
@@ -13,11 +13,13 @@
 SIDE = 4
 OTHERS = (1, 2, 3)
 FAR = ((2, 0), (2, 1))
-NEAR = ((1, 0), (1, 1), (3, 0), (3, 1))
+NEAR = ((1, 0), (3, 0), (1, 1), (3, 1))
+LAST = ((1, 1), (3, 1))
 HERE = ((0, 1), (0, 0))
 
 OWN, RELAY, LEFT, RIGHT, LEFT2, RIGHT2, TARGET, SIGN, LIVE = 0, 8, 32, 48, 64, 80, 96, 112, 128
 PLAN_SIZE = 256
+LATE = 8
 
 
 def shift_tm(value, dy, dx):
@@ -117,12 +119,14 @@
         lax.fori_loop(0, reads, arrivals, 0)
 
         def terms(q, carry):
-            plan[LEFT2 + q] = place[left2[q, worker]]
-            plan[RIGHT2 + q] = place[right2[q, worker]]
+            a, b = place[left2[q, worker]], place[right2[q, worker]]
+            plan[LEFT2 + q] = a
+            plan[RIGHT2 + q] = b
+            late = jnp.logical_or((a >> 1) & 3 == 3, (b >> 1) & 3 == 3).astype(jnp.int32)
             target = ids_ref[q, worker] - time * 8
             ahead = ((target >> 1) - z) & 3
             order = jnp.where(ahead == 2, 0, jnp.where(ahead == 1, 1, jnp.where(ahead == 3, 2, 3)))
-            plan[TARGET + q] = order + ((target + core) & 1) * SIDE
+            plan[TARGET + q] = order + ((target + core) & 1) * SIDE + late * LATE
             plan[SIGN + q] = signs_ref[q, worker]
             return carry
 
@@ -279,28 +283,37 @@
     )(plan, own, *upper_line, *upper_far, *lower_line, *lower_far)
 
 
-def signed_sums(plan, first, targets, pieces, norm):
-    rank, width = pieces[0].shape[1:]
+def signed_sums(plan, late, first, targets, pieces, before, norm):
     count = len(pieces)
+    here = [n for n in range(count) if pieces[n] is not None]
+    given = [pieces[n] for n in here] + list(before)
+    rank, width = given[0].shape[1:]
 
     def kernel(plan_ref, *refs):
-        keep_ref, give_ref, blocks, stacked, sums, sems = refs[count:]
+        keep_ref, give_ref, blocks, stacked, sums, sems = refs[len(given) :]
+        total_ref = sums if before else give_ref
+        pairs = [(refs[n], blocks.at[pl.ds(2 * at, 2)]) for n, at in enumerate(here)]
+        if before:
+            pairs.append((refs[len(here)].at[pl.ds(first, targets)], keep_ref))
+            pairs.append((refs[len(here) + 1].at[pl.ds(first, targets)], sums))
         copies = [
-            pltpu.make_async_copy(refs[n], blocks.at[pl.ds(2 * n, 2)], sems.at[n])
-            for n in range(count)
+            pltpu.make_async_copy(source, target, sems.at[n])
+            for n, (source, target) in enumerate(pairs)
         ]
         for copy in copies:
             copy.start()
-        keep_ref[...] = jnp.zeros_like(keep_ref)
-        sums[...] = jnp.zeros_like(sums)
+        if not before:
+            keep_ref[...] = jnp.zeros_like(keep_ref)
+            give_ref[...] = jnp.zeros_like(give_ref)
         for copy in copies:
             copy.wait()
 
         def pair(index, carry):
-            code = plan_ref[TARGET + index]
+            code = plan_ref[TARGET + index] - late * LATE
             where = (code & 3) - first
-
-            @pl.when(jnp.logical_and(where >= 0, where < targets))
+            wanted = jnp.logical_and(where >= 0, where < targets)
+
+            @pl.when(jnp.logical_and(wanted, jnp.logical_and(code >= 0, code < LATE)))
             def _():
                 stack_right(blocks[plan_ref[RIGHT2 + index]], stacked, rank)
                 product = jnp.dot(
@@ -316,29 +329,34 @@
 
                 @pl.when(code >= SIDE)
                 def _():
-                    sums[where] += term
+                    total_ref[where] += term
 
             return carry
 
         lax.fori_loop(0, plan_ref[LIVE], pair, 0)
-        give_ref[...] = sums[...].astype(give_ref.dtype)
+        if before:
+            give_ref[...] = sums[...].astype(give_ref.dtype)
 
     return pl.pallas_call(
         kernel,
         out_shape=[
             jax.ShapeDtypeStruct((targets, rank, width), jnp.float32),
-            jax.ShapeDtypeStruct((targets, rank, width), jnp.bfloat16),
+            jax.ShapeDtypeStruct(
+                (targets, rank, width), jnp.bfloat16 if before else jnp.float32
+            ),
         ],
-        in_specs=[SMEM] + [ANY] * count,
+        in_specs=[SMEM] + [ANY] * len(given),
         out_specs=[pl.BlockSpec(memory_space=pltpu.VMEM)] * 2,
         scratch_shapes=[
             pltpu.VMEM((2 * count, rank, width), jnp.bfloat16),
             pltpu.VMEM((width, width), jnp.bfloat16),
-            pltpu.VMEM((targets, rank, width), jnp.float32),
-            pltpu.SemaphoreType.DMA((count,)),
+            pltpu.VMEM((targets if before else 1, rank, width), jnp.float32),
+            pltpu.SemaphoreType.DMA((len(given),)),
         ],
-        compiler_params=pltpu.CompilerParams(vmem_limit_bytes=28 << 20),
-    )(plan, *pieces)
+        compiler_params=pltpu.CompilerParams(
+            vmem_limit_bytes=(22 << 20) if before else (28 << 20)
+        ),
+    )(plan, *given)
 
 
 def gather_nodes(node_blocks, plan):
@@ -407,17 +425,23 @@
             arrived[dz, dc] = product if (dz, dc) == (0, 0) else shift_ops(product, dz, dc)
         done += len(part)
 
-    factors = [arrived[dz, dc] for dz in range(SIDE) for dc in range(2)]
-    keep, give = signed_sums(plan, 0, 1, factors, norm)
-    both = keep[0] + shift_ops(give[0], 0, 1).astype(jnp.float32)
-    far = shift_ops(both.astype(jnp.bfloat16), 2, 0)
-    keep, give = signed_sums(plan, 1, 3, factors, norm)
-    both = keep + shift_ops(give, 0, 1).astype(jnp.float32)
-    near = both.astype(jnp.bfloat16)
-    total = both[2] + far.astype(jnp.float32)
-    for n, dz in ((0, 1), (1, 3)):
-        total = total + shift_ops(near[n], dz, 0).astype(jnp.float32)
-    return total[None]
+    offsets = [(dz, dc) for dz in range(SIDE) for dc in range(2)]
+    factors = [arrived[offset] for offset in offsets]
+    ready = [None if offset in LAST else arrived[offset] for offset in offsets]
+    early = signed_sums(plan, 0, 0, SIDE, ready, (), norm)
+
+    def both_cores(first, targets):
+        keep, give = signed_sums(plan, 1, first, targets, factors, early, norm)
+        return keep + shift_ops(give, 0, 1).astype(jnp.float32)
+
+    far = both_cores(0, 1).astype(jnp.bfloat16)
+    parts = [shift_ops(far[0], 2, 0)]
+    near = both_cores(1, 2).astype(jnp.bfloat16)
+    parts += [shift_ops(near[0], 1, 0), shift_ops(near[1], 3, 0)]
+    total = both_cores(3, 1)
+    for part in parts:
+        total = total + part.astype(jnp.float32)[None]
+    return total
 
 
 def solution(mesh):

time: 279 us -> 277 us (level)
  starting transfers between devices: 82.4 us -> 75.1 us
  Pallas kernels: 35.1 us -> 41.7 us
  waiting for transfers between devices: 156 us -> 153 us
    ppermute x12 -> x13, starting transfers between devices: 52.9 us -> 45.7 us  [shift_ops(): return lax.ppermute(value, 'ops', pairs)]
    pallas_call x2 -> x4, Pallas kernels: 12.4 us -> 18.9 us  [signed_sums(): pl.pallas_call(kernel, out_shape=[jax.ShapeDtypeStruct((targets, rank, wi...]
    ppermute x12 -> x13, waiting for transfers between devices: 84 us -> 81.3 us  [shift_ops(): return lax.ppermute(value, 'ops', pairs)]
  transfers between devices with their start and end apart: 36 -> 37, of which waited for: 18 -> 16; matrix products, arithmetic and copies ran while one was open for 0% -> 0% of each run, Pallas kernels for 7% -> 11%
where the time goes in v2:
time: 277 us; the launch traced here: 274 us
  waiting for transfers between devices  153 us (55%)
  starting transfers between devices  75.1 us (27%)
  Pallas kernels  41.7 us (15%)
    ppermute x13, waiting for transfers between devices, shift_ops(): return lax.ppermute(value, 'ops', pairs)  81.3 us
    ppermute x24, waiting for transfers between devices, shift_tm(): return lax.ppermute(value, 'tm', pairs)  71.8 us
    ppermute x13, starting transfers between devices, shift_ops(): return lax.ppermute(value, 'ops', pairs)  45.7 us
    ppermute x24, starting transfers between devices, shift_tm(): return lax.ppermute(value, 'tm', pairs)  29.4 us
    pallas_call x4, Pallas kernels, signed_sums(): pl.pallas_call(kernel, out_shape=[jax.ShapeDtypeStruct((targets, rank, wi...  18.9 us
    pallas_call x3, Pallas kernels, pair_products(): pl.pallas_call(kernel, out_shape=[jax.ShapeDtypeStruct((2, rank, width),...  13.9 us
  transfers between devices with their start and end apart: 37, of which 16 were waited for; matrix products, arithmetic and copies ran while one was open for 0% of the time, Pallas kernels for 11%

profile of v2, /device:TPU:1, one launch (start us, length us, event | category | flops | bytes accessed | tf_op | source)
XLA Modules:
  0.0 273.9 jit_solution(3970017292082663482)
XLA Ops:
  0.1 1.8 fusion.1
  1.9 2.2 collective-permute-start.9
  4.1 1.5 collective-permute-start.12
  5.6 1.2 collective-permute-start.3
  6.8 1.5 collective-permute-start.6
  8.3 10.2 %collective-permute-done.9.refs_6_ = bf16[2,192,768]{2,1,0:T(8,128)(2,1)S(1)} collective-permute-done((bf16[2,192,768]{2,1,0:T(8,128)(2,1)S(1)}, bf16[2,192,768]{2,1,0:T(8,128)(2,1)S(1)}, u32[]{:S(2)}, u32[]{:S(2)}) %collective-permute-start.9) | collective-permute-done | bytes 589856 | tf_op jit(solution)/shard_map/ppermute | solution.py:31
  18.5 1.3 collective-permute-start.14
  19.7 1.2 collective-permute-start.4
  21.0 1.5 collective-permute-start.8
  22.4 0.2 collective-permute-start.11
  22.6 8.5 %collective-permute-done.10.refs_7_ = bf16[2,192,768]{2,1,0:T(8,128)(2,1)S(1)} collective-permute-done((bf16[2,192,768]{2,1,0:T(8,128)(2,1)S(1)}, bf16[2,192,768]{2,1,0:T(8,128)(2,1)S(1)}, u32[]{:S(2)}, u32[]{:S(2)}) %collective-permute-start.10) | collective-permute-done | bytes 589856 | tf_op jit(solution)/shard_map/ppermute | solution.py:31
  31.1 1.3 collective-permute-start.13
  32.4 1.2 collective-permute-start.5
  33.6 1.5 collective-permute-start.7
  35.1 5.2 %make_plan.1.plan_ref = s32[256]{0:T(256)S(1)} custom-call(s32[16,128]{1,0:T(8,128)S(1)} %bitcast.25, s32[24,128]{1,0:T(8,128)S(1)} %bitcast.23, s32[24,128]{1,0:T(8,128)S(1)} %bitcast.24, s32[16,128]{1,0:T(8,128)S(1)} %bitcast.26, s32[16,128]{1,0:T(8,128)S(1)} %bitcast.27, s32[16,128]{1,0:T(8,128)S(1)} %bitcast.28, s32[128]{0:T(128)S(1)} %copy-done.9, ...), custom_call_target="tpu_custom_call" | custom-call | tf_op jit(solution)/shard_map/make_plan/pallas_call | solution.py:136
  40.3 3.4 %collective-permute-done.11.refs_8_ = bf16[2,192,768]{2,1,0:T(8,128)(2,1)S(1)} collective-permute-done((bf16[2,192,768]{2,1,0:T(8,128)(2,1)S(1)}, bf16[2,192,768]{2,1,0:T(8,128)(2,1)S(1)}, u32[]{:S(2)}, u32[]{:S(2)}) %collective-permute-start.11) | collective-permute-done | bytes 589856 | tf_op jit(solution)/shard_map/ppermute | solution.py:31
  43.7 1.8 collective-permute-done.5.refs_2_
  45.5 2.6 pick_relayed.1
  48.1 0.6 collective-permute-start.15
  48.7 1.1 pick_own.1
  49.9 0.7 collective-permute-start
  50.5 2.7 collective-permute-start.1
  53.3 0.9 collective-permute-start.18
  54.2 2.6 collective-permute-start.19
  56.8 16.9 %collective-permute-done.refs_1_ = bf16[1,192,768]{2,1,0:T(8,128)(2,1)S(1)} collective-permute-done((bf16[1,192,768]{2,1,0:T(8,128)(2,1)S(1)}, bf16[1,192,768]{2,1,0:T(8,128)(2,1)S(1)}, u32[]{:S(2)}, u32[]{:S(2)}) %collective-permute-start) | collective-permute-done | bytes 294944 | tf_op jit(solution)/shard_map/ppermute | solution.py:31
  73.7 4.9 %collective-permute-done.1.refs_2_ = bf16[1,192,768]{2,1,0:T(8,128)(2,1)S(1)} collective-permute-done((bf16[1,192,768]{2,1,0:T(8,128)(2,1)S(1)}, bf16[1,192,768]{2,1,0:T(8,128)(2,1)S(1)}, u32[]{:S(2)}, u32[]{:S(2)}) %collective-permute-start.1) | collective-permute-done | bytes 294944 | tf_op jit(solution)/shard_map/ppermute | solution.py:31
  78.6 2.2 collective-permute-start.20
  80.8 1.6 collective-permute-start.16
  82.6 1.9 collective-permute-done.20.refs_10_
  84.5 1.9 collective-permute-start.22
  86.4 1.5 collective-permute-start.23
  87.9 6.3 %collective-permute-done.16.refs_6_ = bf16[3,192,768]{2,1,0:T(8,128)(2,1)S(1)} collective-permute-done((bf16[3,192,768]{2,1,0:T(8,128)(2,1)S(1)}, bf16[3,192,768]{2,1,0:T(8,128)(2,1)S(1)}, u32[]{:S(2)}, u32[]{:S(2)}) %collective-permute-start.16) | collective-permute-done | bytes 884768 | tf_op jit(solution)/shard_map/ppermute | solution.py:31
  94.2 16.4 %collective-permute-done.17.refs_7_ = bf16[3,192,768]{2,1,0:T(8,128)(2,1)S(1)} collective-permute-done((bf16[3,192,768]{2,1,0:T(8,128)(2,1)S(1)}, bf16[3,192,768]{2,1,0:T(8,128)(2,1)S(1)}, u32[]{:S(2)}, u32[]{:S(2)}) %collective-permute-start.17) | collective-permute-done | bytes 884768 | tf_op jit(solution)/shard_map/ppermute | solution.py:31
  110.6 1.5 collective-permute-done.23.refs_14_
  112.1 4.0 %pair_products.5 = (bf16[2,384,768]{2,1,0:T(8,128)(2,1)S(1)}, bf16[2,384,768]{2,1,0:T(8,128)(2,1)S(1)}) custom-call(s32[256]{0:T(256)S(1)} %make_plan.1.plan_ref, bf16[384,768]{1,0:T(8,128)(2,1)S(1)} %get-tuple-element.36.refs_0_, bf16[1,192,768]{2,1,0:T(8,128)(2,1)S(1)} %collective-permute-done.refs_1_, ...), custom_call_target="tpu_custom_call" | custom-call | tf_op jit(solution)/shard_map/pair_products/pallas_call | solution.py:270
  116.1 3.3 %collective-permute-start.27 = (bf16[2,384,768]{2,1,0:T(8,128)(2,1)S(1)}, bf16[2,384,768]{2,1,0:T(8,128)(2,1)S(1)}, u32[]{:S(2)}, u32[]{:S(2)}) collective-permute-start(bf16[2,384,768]{2,1,0:T(8,128)(2,1)S(1)} %get-tuple-element.55), channel_id=1, source_target_pairs={{0,4},{1,5},{2,6},{3,7},{4,0},{5,1},{6,2},{7,3},{8,12},{9,13},{10,... | collective-permute-start | bytes 3538952 | tf_op jit(solution)/shard_map/ppermute | solution.py:40
  119.5 19.1 %collective-permute-start.28 = (bf16[2,384,768]{2,1,0:T(8,128)(2,1)S(1)}, bf16[2,384,768]{2,1,0:T(8,128)(2,1)S(1)}, u32[]{:S(2)}, u32[]{:S(2)}) collective-permute-start(bf16[2,384,768]{2,1,0:T(8,128)(2,1)S(1)} %get-tuple-element.56), channel_id=1, source_target_pairs={{0,5},{1,4},{2,7},{3,6},{4,1},{5,0},{6,3},{7,2},{8,13},{9,12},{10,... | collective-permute-start | bytes 3538952 | tf_op jit(solution)/shard_map/ppermute | solution.py:40
  138.6 5.9 %pair_products.4 = (bf16[2,384,768]{2,1,0:T(8,128)(2,1)S(1)}, bf16[2,384,768]{2,1,0:T(8,128)(2,1)S(1)}, bf16[2,384,768]{2,1,0:T(8,128)(2,1)S(1)}, bf16[2,384,768]{2,1,0:T(8,128)(2,1)S(1)}) custom-call(s32[256]{0:T(256)S(1)} %make_plan.1.plan_ref, bf16[384,768]{1,0:T(8,128)(2,1)S(1)} %get-tuple-element.36.refs_0_, ...), custom_call_target="tpu_custom_call" | custom-call | tf_op jit(solution)/shard_map/pair_products/pallas_call | solution.py:270
  144.6 1.3 collective-permute-start.25
  145.8 2.2 collective-permute-start.29
  148.0 4.0 %pair_products.3 = (bf16[2,384,768]{2,1,0:T(8,128)(2,1)S(1)}, bf16[2,384,768]{2,1,0:T(8,128)(2,1)S(1)}) custom-call(s32[256]{0:T(256)S(1)} %make_plan.1.plan_ref, bf16[384,768]{1,0:T(8,128)(2,1)S(1)} %get-tuple-element.36.refs_0_, bf16[1,192,768]{2,1,0:T(8,128)(2,1)S(1)} %collective-permute-done.refs_1_, ...), custom_call_target="tpu_custom_call" | custom-call | tf_op jit(solution)/shard_map/pair_products/pallas_call | solution.py:270
  152.0 0.2 collective-permute-start.24
  152.3 13.7 %collective-permute-start.26 = (bf16[2,384,768]{2,1,0:T(8,128)(2,1)S(1)}, bf16[2,384,768]{2,1,0:T(8,128)(2,1)S(1)}, u32[]{:S(2)}, u32[]{:S(2)}) collective-permute-start(bf16[2,384,768]{2,1,0:T(8,128)(2,1)S(1)} %get-tuple-element.54), channel_id=1, source_target_pairs={{0,3},{1,2},{2,5},{3,4},{4,7},{5,6},{6,1},{7,0},{8,11},{9,10},{10,... | collective-permute-start | bytes 3538952 | tf_op jit(solution)/shard_map/ppermute | solution.py:40
  165.9 21.5 %collective-permute-done.28.refs_4_.refs_5_ = bf16[2,384,768]{2,1,0:T(8,128)(2,1)S(1)} collective-permute-done((bf16[2,384,768]{2,1,0:T(8,128)(2,1)S(1)}, bf16[2,384,768]{2,1,0:T(8,128)(2,1)S(1)}, u32[]{:S(2)}, u32[]{:S(2)}) %collective-permute-start.28) | collective-permute-done | bytes 1179680 | tf_op jit(solution)/shard_map/ppermute | solution.py:40
  187.4 1.1 collective-permute-start.30
  188.5 14.7 %collective-permute-done.25.refs_2_ = bf16[2,384,768]{2,1,0:T(8,128)(2,1)S(1)} collective-permute-done((bf16[2,384,768]{2,1,0:T(8,128)(2,1)S(1)}, bf16[2,384,768]{2,1,0:T(8,128)(2,1)S(1)}, u32[]{:S(2)}, u32[]{:S(2)}) %collective-permute-start.25) | collective-permute-done | bytes 1179680 | tf_op jit(solution)/shard_map/ppermute | solution.py:40
  203.3 6.0 %shard_map.100 = (f32[4,384,768]{2,1,0:T(8,128)S(1)}, f32[4,384,768]{2,1,0:T(8,128)S(1)}) custom-call(s32[256]{0:T(256)S(1)} %make_plan.1.plan_ref, bf16[2,384,768]{2,1,0:T(8,128)(2,1)S(1)} %get-tuple-element.51.refs_0_, bf16[2,384,768]{2,1,0:T(8,128)(2,1)S(1)} %collective-permute-done.24.refs_1_, bf16[2,384,768]{2,1,0:T(8,128)(2,1)S(1)} %collective-permute-done.25.refs_2_, ...), custom_call_target="tpu_custom_call" | custom-call | tf_op jit(solution)/shard_map/pallas_call | solution.py:340
  209.2 19.3 %collective-permute-done.26.refs_3_ = bf16[2,384,768]{2,1,0:T(8,128)(2,1)S(1)} collective-permute-done((bf16[2,384,768]{2,1,0:T(8,128)(2,1)S(1)}, bf16[2,384,768]{2,1,0:T(8,128)(2,1)S(1)}, u32[]{:S(2)}, u32[]{:S(2)}) %collective-permute-start.26) | collective-permute-done | bytes 1179680 | tf_op jit(solution)/shard_map/ppermute | solution.py:40
  228.5 0.7 collective-permute-done.30.refs_7_
  229.3 3.9 %shard_map.103 = (f32[2,384,768]{2,1,0:T(8,128)S(1)}, bf16[2,384,768]{2,1,0:T(8,128)(2,1)S(1)}) custom-call(s32[256]{0:T(256)S(1)} %make_plan.1.plan_ref, bf16[2,384,768]{2,1,0:T(8,128)(2,1)S(1)} %get-tuple-element.51.refs_0_, bf16[2,384,768]{2,1,0:T(8,128)(2,1)S(1)} %collective-permute-done.24.refs_1_, ...), custom_call_target="tpu_custom_call" | custom-call | tf_op jit(solution)/shard_map/pallas_call | solution.py:340
  233.2 0.1 collective-permute-start.34
  233.3 3.2 %shard_map.102 = (f32[1,384,768]{2,1,0:T(8,128)S(1)}, bf16[1,384,768]{2,1,0:T(8,128)(2,1)S(1)}) custom-call(s32[256]{0:T(256)S(1)} %make_plan.1.plan_ref, bf16[2,384,768]{2,1,0:T(8,128)(2,1)S(1)} %get-tuple-element.51.refs_0_, bf16[2,384,768]{2,1,0:T(8,128)(2,1)S(1)} %collective-permute-done.24.refs_1_, ...), custom_call_target="tpu_custom_call" | custom-call | tf_op jit(solution)/shard_map/pallas_call | solution.py:340
  236.5 0.5 collective-permute-start.32
  237.0 5.8 %shard_map.101 = (f32[1,384,768]{2,1,0:T(8,128)S(1)}, bf16[1,384,768]{2,1,0:T(8,128)(2,1)S(1)}) custom-call(s32[256]{0:T(256)S(1)} %make_plan.1.plan_ref, bf16[2,384,768]{2,1,0:T(8,128)(2,1)S(1)} %get-tuple-element.51.refs_0_, bf16[2,384,768]{2,1,0:T(8,128)(2,1)S(1)} %collective-permute-done.24.refs_1_, ...), custom_call_target="tpu_custom_call" | custom-call | tf_op jit(solution)/shard_map/pallas_call | solution.py:340
  242.8 0.1 collective-permute-start.31
  242.9 0.1 fusion
  243.1 0.9 collective-permute-start.33
  244.0 0.3 add_convert_fusion
  244.3 0.1 slice_bitcast_fusion.1
  244.4 1.9 collective-permute-start.35
  246.3 1.3 collective-permute-start.36
  247.6 11.5 %collective-permute-done.33 = bf16[384,768]{1,0:T(8,128)(2,1)S(1)} collective-permute-done((bf16[384,768]{1,0:T(8,128)(2,1)S(1)}, bf16[384,768]{1,0:T(8,128)(2,1)S(1)}, u32[]{:S(2)}, u32[]{:S(2)}) %collective-permute-start.33) | collective-permute-done | bytes 589856 | tf_op jit(solution)/shard_map/ppermute | solution.py:40
  259.1 13.5 %collective-permute-done.35 = bf16[384,768]{1,0:T(8,128)(2,1)S(1)} collective-permute-done((bf16[384,768]{1,0:T(8,128)(2,1)S(1)}, bf16[384,768]{1,0:T(8,128)(2,1)S(1)}, u32[]{:S(2)}, u32[]{:S(2)}) %collective-permute-start.35) | collective-permute-done | bytes 589856 | tf_op jit(solution)/shard_map/ppermute | solution.py:40
  272.6 1.4 convert_add_fusion
  (45 shorter events, 0.2 us)
Async XLA Ops:
  0.0 35.1 %copy-start.3 = (s32[128,16]{0,1:T(8,128)S(1)}, s32[128,16]{0,1:T(8,128)}, u32[]{:S(2)}) copy-start(s32[128,16]{0,1:T(8,128)} %param.12) | copy-start | bytes 24580
  0.0 35.1 %copy-start.1 = (s32[128,24]{0,1:T(8,128)S(1)}, s32[128,24]{0,1:T(8,128)}, u32[]{:S(2)}) copy-start(s32[128,24]{0,1:T(8,128)} %param.13) | copy-start | bytes 36868
  0.0 35.1 %copy-start.2 = (s32[128,24]{0,1:T(8,128)S(1)}, s32[128,24]{0,1:T(8,128)}, u32[]{:S(2)}) copy-start(s32[128,24]{0,1:T(8,128)} %param.14) | copy-start | bytes 36868
  0.0 35.1 %copy-start.4 = (s32[128,16]{0,1:T(8,128)S(1)}, s32[128,16]{0,1:T(8,128)}, u32[]{:S(2)}) copy-start(s32[128,16]{0,1:T(8,128)} %param.15) | copy-start | bytes 24580
  0.0 35.1 %copy-start.5 = (s32[128,16]{0,1:T(8,128)S(1)}, s32[128,16]{0,1:T(8,128)}, u32[]{:S(2)}) copy-start(s32[128,16]{0,1:T(8,128)} %param.16) | copy-start | bytes 24580
  0.0 35.1 %copy-start.6 = (s32[128,16]{0,1:T(8,128)S(1)}, s32[128,16]{0,1:T(8,128)}, u32[]{:S(2)}) copy-start(s32[128,16]{0,1:T(8,128)} %param.17) | copy-start | bytes 24580
  0.0 35.1 %copy-start.7 = (s32[128,16]{0,1:T(8,128)S(1)}, s32[128,16]{0,1:T(8,128)}, u32[]{:S(2)}) copy-start(s32[128,16]{0,1:T(8,128)} %param.19) | copy-start | bytes 24580
  0.0 35.1 %copy-start.8 = (s32[128,16]{0,1:T(8,128)S(1)}, s32[128,16]{0,1:T(8,128)}, u32[]{:S(2)}) copy-start(s32[128,16]{0,1:T(8,128)} %param.20) | copy-start | bytes 24580
  0.1 35.1 %copy-start.9 = (s32[128]{0:T(128)S(1)}, s32[128]{0:T(128)}, u32[]{:S(2)}) copy-start(s32[128]{0:T(128)} %live2.1) | copy-start | bytes 1540
  1.9 16.5 %collective-permute-start.9 = (bf16[2,192,768]{2,1,0:T(8,128)(2,1)S(1)}, bf16[2,192,768]{2,1,0:T(8,128)(2,1)S(1)}, u32[]{:S(2)}, u32[]{:S(2)}) collective-permute-start(bf16[2,192,768]{2,1,0:T(8,128)(2,1)S(1)} %get-tuple-element.70), channel_id=1, source_target_pairs={{0,32},{8,40},{16,48},{24,56},{32,64},{40,72},{48,80},{56,88},{64,... | collective-permute-start | bytes 1769480 | tf_op jit(solution)/shard_map/ppermute | solution.py:31
  4.1 15.7 %collective-permute-start.12 = (bf16[2,192,768]{2,1,0:T(8,128)(2,1)S(1)}, bf16[2,192,768]{2,1,0:T(8,128)(2,1)S(1)}, u32[]{:S(2)}, u32[]{:S(2)}) collective-permute-start(bf16[2,192,768]{2,1,0:T(8,128)(2,1)S(1)} %get-tuple-element.67), channel_id=1, source_target_pairs={{0,96},{8,104},{16,112},{24,120},{32,0},{40,8},{48,16},{56,24},{64... | collective-permute-start | bytes 1769480 | tf_op jit(solution)/shard_map/ppermute | solution.py:31
  5.6 15.3 %collective-permute-start.3 = (bf16[2,192,768]{2,1,0:T(8,128)(2,1)S(1)}, bf16[2,192,768]{2,1,0:T(8,128)(2,1)S(1)}, u32[]{:S(2)}, u32[]{:S(2)}) collective-permute-start(bf16[2,192,768]{2,1,0:T(8,128)(2,1)S(1)} %get-tuple-element.69), channel_id=1, source_target_pairs={{0,8},{8,16},{16,24},{24,0},{32,40},{40,48},{48,56},{56,32},{64,72... | collective-permute-start | bytes 1769480 | tf_op jit(solution)/shard_map/ppermute | solution.py:31
  6.8 15.6 %collective-permute-start.6 = (bf16[2,192,768]{2,1,0:T(8,128)(2,1)S(1)}, bf16[2,192,768]{2,1,0:T(8,128)(2,1)S(1)}, u32[]{:S(2)}, u32[]{:S(2)}) collective-permute-start(bf16[2,192,768]{2,1,0:T(8,128)(2,1)S(1)} %get-tuple-element.68), channel_id=1, source_target_pairs={{0,24},{8,0},{16,8},{24,16},{32,56},{40,32},{48,40},{56,48},{64,88... | collective-permute-start | bytes 1769480 | tf_op jit(solution)/shard_map/ppermute | solution.py:31
  8.3 22.8 %collective-permute-start.10 = (bf16[2,192,768]{2,1,0:T(8,128)(2,1)S(1)}, bf16[2,192,768]{2,1,0:T(8,128)(2,1)S(1)}, u32[]{:S(2)}, u32[]{:S(2)}) collective-permute-start(bf16[2,192,768]{2,1,0:T(8,128)(2,1)S(1)} %get-tuple-element.67), channel_id=1, source_target_pairs={{0,32},{8,40},{16,48},{24,56},{32,64},{40,72},{48,80},{56,88},{64,... | collective-permute-start | bytes 1769480 | tf_op jit(solution)/shard_map/ppermute | solution.py:31
  18.5 13.9 %collective-permute-start.14 = (bf16[2,192,768]{2,1,0:T(8,128)(2,1)S(1)}, bf16[2,192,768]{2,1,0:T(8,128)(2,1)S(1)}, u32[]{:S(2)}, u32[]{:S(2)}) collective-permute-start(bf16[2,192,768]{2,1,0:T(8,128)(2,1)S(1)} %get-tuple-element.70), channel_id=1, source_target_pairs={{0,96},{8,104},{16,112},{24,120},{32,0},{40,8},{48,16},{56,24},{64... | collective-permute-start | bytes 1769480 | tf_op jit(solution)/shard_map/ppermute | solution.py:31
  19.7 13.9 %collective-permute-start.4 = (bf16[2,192,768]{2,1,0:T(8,128)(2,1)S(1)}, bf16[2,192,768]{2,1,0:T(8,128)(2,1)S(1)}, u32[]{:S(2)}, u32[]{:S(2)}) collective-permute-start(bf16[2,192,768]{2,1,0:T(8,128)(2,1)S(1)} %get-tuple-element.68), channel_id=1, source_target_pairs={{0,8},{8,16},{16,24},{24,0},{32,40},{40,48},{48,56},{56,32},{64,72... | collective-permute-start | bytes 1769480 | tf_op jit(solution)/shard_map/ppermute | solution.py:31
  21.0 19.3 %collective-permute-start.8 = (bf16[2,192,768]{2,1,0:T(8,128)(2,1)S(1)}, bf16[2,192,768]{2,1,0:T(8,128)(2,1)S(1)}, u32[]{:S(2)}, u32[]{:S(2)}) collective-permute-start(bf16[2,192,768]{2,1,0:T(8,128)(2,1)S(1)} %get-tuple-element.69), channel_id=1, source_target_pairs={{0,24},{8,0},{16,8},{24,16},{32,56},{40,32},{48,40},{56,48},{64,88... | collective-permute-start | bytes 1769480 | tf_op jit(solution)/shard_map/ppermute | solution.py:31
  22.4 21.3 %collective-permute-start.11 = (bf16[2,192,768]{2,1,0:T(8,128)(2,1)S(1)}, bf16[2,192,768]{2,1,0:T(8,128)(2,1)S(1)}, u32[]{:S(2)}, u32[]{:S(2)}) collective-permute-start(bf16[2,192,768]{2,1,0:T(8,128)(2,1)S(1)} %collective-permute-done.9.refs_6_), channel_id=1, source_target_pairs={{0,32},{8,40},{16,48},{24,56},{32,64},{40,72},{48,80},{56,88},{64,... | collective-permute-start | bytes 1769480 | tf_op jit(solution)/shard_map/ppermute | solution.py:31
  31.1 12.6 %collective-permute-start.13 = (bf16[2,192,768]{2,1,0:T(8,128)(2,1)S(1)}, bf16[2,192,768]{2,1,0:T(8,128)(2,1)S(1)}, u32[]{:S(2)}, u32[]{:S(2)}) collective-permute-start(bf16[2,192,768]{2,1,0:T(8,128)(2,1)S(1)} %collective-permute-done.12.refs_11_), channel_id=1, source_target_pairs={{0,96},{8,104},{16,112},{24,120},{32,0},{40,8},{48,16},{56,24},{64... | collective-permute-start | bytes 1769480 | tf_op jit(solution)/shard_map/ppermute | solution.py:31
  32.4 13.2 %collective-permute-start.5 = (bf16[2,192,768]{2,1,0:T(8,128)(2,1)S(1)}, bf16[2,192,768]{2,1,0:T(8,128)(2,1)S(1)}, u32[]{:S(2)}, u32[]{:S(2)}) collective-permute-start(bf16[2,192,768]{2,1,0:T(8,128)(2,1)S(1)} %collective-permute-done.3.refs_0_), channel_id=1, source_target_pairs={{0,8},{8,16},{16,24},{24,0},{32,40},{40,48},{48,56},{56,32},{64,72... | collective-permute-start | bytes 1769480 | tf_op jit(solution)/shard_map/ppermute | solution.py:31
  33.6 11.9 %collective-permute-start.7 = (bf16[2,192,768]{2,1,0:T(8,128)(2,1)S(1)}, bf16[2,192,768]{2,1,0:T(8,128)(2,1)S(1)}, u32[]{:S(2)}, u32[]{:S(2)}) collective-permute-start(bf16[2,192,768]{2,1,0:T(8,128)(2,1)S(1)} %collective-permute-done.6.refs_5_), channel_id=1, source_target_pairs={{0,24},{8,0},{16,8},{24,16},{32,56},{40,32},{48,40},{56,48},{64,88... | collective-permute-start | bytes 1769480 | tf_op jit(solution)/shard_map/ppermute | solution.py:31
  45.5 3.2 %copy-start = (bf16[4,384,768]{2,1,0:T(8,128)(2,1)S(1)}, bf16[4,384,768]{2,1,0:T(8,128)(2,1)}, u32[]{:S(2)}) copy-start(bf16[4,384,768]{2,1,0:T(8,128)(2,1)} %nodes_ref.1) | copy-start | bytes 7077892
  48.1 38.3 %collective-permute-start.15 = (bf16[3,192,768]{2,1,0:T(8,128)(2,1)S(1)}, bf16[3,192,768]{2,1,0:T(8,128)(2,1)S(1)}, u32[]{:S(2)}, u32[]{:S(2)}) collective-permute-start(bf16[3,192,768]{2,1,0:T(8,128)(2,1)S(1)} %get-tuple-element.41), channel_id=1, source_target_pairs={{0,32},{8,40},{16,48},{24,56},{32,64},{40,72},{48,80},{56,88},{64,... | collective-permute-start | bytes 2654216 | tf_op jit(solution)/shard_map/ppermute | solution.py:31
  49.9 23.8 %collective-permute-start = (bf16[1,192,768]{2,1,0:T(8,128)(2,1)S(1)}, bf16[1,192,768]{2,1,0:T(8,128)(2,1)S(1)}, u32[]{:S(2)}, u32[]{:S(2)}) collective-permute-start(bf16[1,192,768]{2,1,0:T(8,128)(2,1)S(1)} %get-tuple-element.37), channel_id=1, source_target_pairs={{0,32},{8,40},{16,48},{24,56},{32,64},{40,72},{48,80},{56,88},{64,... | collective-permute-start | bytes 884744 | tf_op jit(solution)/shard_map/ppermute | solution.py:31
  50.5 28.1 %collective-permute-start.1 = (bf16[1,192,768]{2,1,0:T(8,128)(2,1)S(1)}, bf16[1,192,768]{2,1,0:T(8,128)(2,1)S(1)}, u32[]{:S(2)}, u32[]{:S(2)}) collective-permute-start(bf16[1,192,768]{2,1,0:T(8,128)(2,1)S(1)} %get-tuple-element.38), channel_id=1, source_target_pairs={{0,64},{8,72},{16,80},{24,88},{32,96},{40,104},{48,112},{56,120},{... | collective-permute-start | bytes 884744 | tf_op jit(solution)/shard_map/ppermute | solution.py:31
  53.3 27.6 %collective-permute-start.18 = (bf16[1,192,768]{2,1,0:T(8,128)(2,1)S(1)}, bf16[1,192,768]{2,1,0:T(8,128)(2,1)S(1)}, u32[]{:S(2)}, u32[]{:S(2)}) collective-permute-start(bf16[1,192,768]{2,1,0:T(8,128)(2,1)S(1)} %get-tuple-element.44), channel_id=1, source_target_pairs={{0,8},{8,16},{16,24},{24,0},{32,40},{40,48},{48,56},{56,32},{64,72... | collective-permute-start | bytes 884744 | tf_op jit(solution)/shard_map/ppermute | solution.py:31
  54.2 28.3 %collective-permute-start.19 = (bf16[1,192,768]{2,1,0:T(8,128)(2,1)S(1)}, bf16[1,192,768]{2,1,0:T(8,128)(2,1)S(1)}, u32[]{:S(2)}, u32[]{:S(2)}) collective-permute-start(bf16[1,192,768]{2,1,0:T(8,128)(2,1)S(1)} %get-tuple-element.45), channel_id=1, source_target_pairs={{0,16},{8,24},{16,0},{24,8},{32,48},{40,56},{48,32},{56,40},{64,80... | collective-permute-start | bytes 884744 | tf_op jit(solution)/shard_map/ppermute | solution.py:31
  73.7 8.8 %collective-permute-start.2 = (bf16[1,192,768]{2,1,0:T(8,128)(2,1)S(1)}, bf16[1,192,768]{2,1,0:T(8,128)(2,1)S(1)}, u32[]{:S(2)}, u32[]{:S(2)}) collective-permute-start(bf16[1,192,768]{2,1,0:T(8,128)(2,1)S(1)} %get-tuple-element.39), channel_id=1, source_target_pairs={{0,96},{8,104},{16,112},{24,120},{32,0},{40,8},{48,16},{56,24},{64... | collective-permute-start | bytes 884744 | tf_op jit(solution)/shard_map/ppermute | solution.py:31
  78.6 5.9 %collective-permute-start.20 = (bf16[1,192,768]{2,1,0:T(8,128)(2,1)S(1)}, bf16[1,192,768]{2,1,0:T(8,128)(2,1)S(1)}, u32[]{:S(2)}, u32[]{:S(2)}) collective-permute-start(bf16[1,192,768]{2,1,0:T(8,128)(2,1)S(1)} %get-tuple-element.46), channel_id=1, source_target_pairs={{0,24},{8,0},{16,8},{24,16},{32,56},{40,32},{48,40},{56,48},{64,88... | collective-permute-start | bytes 884744 | tf_op jit(solution)/shard_map/ppermute | solution.py:31
  80.8 13.4 %collective-permute-start.16 = (bf16[3,192,768]{2,1,0:T(8,128)(2,1)S(1)}, bf16[3,192,768]{2,1,0:T(8,128)(2,1)S(1)}, u32[]{:S(2)}, u32[]{:S(2)}) collective-permute-start(bf16[3,192,768]{2,1,0:T(8,128)(2,1)S(1)} %get-tuple-element.42), channel_id=1, source_target_pairs={{0,64},{8,72},{16,80},{24,88},{32,96},{40,104},{48,112},{56,120},{... | collective-permute-start | bytes 2654216 | tf_op jit(solution)/shard_map/ppermute | solution.py:31
  82.5 28.2 %collective-permute-start.17 = (bf16[3,192,768]{2,1,0:T(8,128)(2,1)S(1)}, bf16[3,192,768]{2,1,0:T(8,128)(2,1)S(1)}, u32[]{:S(2)}, u32[]{:S(2)}) collective-permute-start(bf16[3,192,768]{2,1,0:T(8,128)(2,1)S(1)} %get-tuple-element.43), channel_id=1, source_target_pairs={{0,96},{8,104},{16,112},{24,120},{32,0},{40,8},{48,16},{56,24},{64... | collective-permute-start | bytes 2654216 | tf_op jit(solution)/shard_map/ppermute | solution.py:31
  82.5 28.2 %collective-permute-start.21 = (bf16[3,192,768]{2,1,0:T(8,128)(2,1)S(1)}, bf16[3,192,768]{2,1,0:T(8,128)(2,1)S(1)}, u32[]{:S(2)}, u32[]{:S(2)}) collective-permute-start(bf16[3,192,768]{2,1,0:T(8,128)(2,1)S(1)} %get-tuple-element.48), channel_id=1, source_target_pairs={{0,8},{8,16},{16,24},{24,0},{32,40},{40,48},{48,56},{56,32},{64,72... | collective-permute-start | bytes 2654216 | tf_op jit(solution)/shard_map/ppermute | solution.py:31
  84.5 26.1 %collective-permute-start.22 = (bf16[3,192,768]{2,1,0:T(8,128)(2,1)S(1)}, bf16[3,192,768]{2,1,0:T(8,128)(2,1)S(1)}, u32[]{:S(2)}, u32[]{:S(2)}) collective-permute-start(bf16[3,192,768]{2,1,0:T(8,128)(2,1)S(1)} %get-tuple-element.49), channel_id=1, source_target_pairs={{0,16},{8,24},{16,0},{24,8},{32,48},{40,56},{48,32},{56,40},{64,80... | collective-permute-start | bytes 2654216 | tf_op jit(solution)/shard_map/ppermute | solution.py:31
  86.4 25.7 %collective-permute-start.23 = (bf16[3,192,768]{2,1,0:T(8,128)(2,1)S(1)}, bf16[3,192,768]{2,1,0:T(8,128)(2,1)S(1)}, u32[]{:S(2)}, u32[]{:S(2)}) collective-permute-start(bf16[3,192,768]{2,1,0:T(8,128)(2,1)S(1)} %get-tuple-element.50), channel_id=1, source_target_pairs={{0,24},{8,0},{16,8},{24,16},{32,56},{40,32},{48,40},{56,48},{64,88... | collective-permute-start | bytes 2654216 | tf_op jit(solution)/shard_map/ppermute | solution.py:31
  116.1 36.1 %collective-permute-start.27 = (bf16[2,384,768]{2,1,0:T(8,128)(2,1)S(1)}, bf16[2,384,768]{2,1,0:T(8,128)(2,1)S(1)}, u32[]{:S(2)}, u32[]{:S(2)}) collective-permute-start(bf16[2,384,768]{2,1,0:T(8,128)(2,1)S(1)} %get-tuple-element.55), channel_id=1, source_target_pairs={{0,4},{1,5},{2,6},{3,7},{4,0},{5,1},{6,2},{7,3},{8,12},{9,13},{10,... | collective-permute-start | bytes 3538952 | tf_op jit(solution)/shard_map/ppermute | solution.py:40
  119.5 67.9 %collective-permute-start.28 = (bf16[2,384,768]{2,1,0:T(8,128)(2,1)S(1)}, bf16[2,384,768]{2,1,0:T(8,128)(2,1)S(1)}, u32[]{:S(2)}, u32[]{:S(2)}) collective-permute-start(bf16[2,384,768]{2,1,0:T(8,128)(2,1)S(1)} %get-tuple-element.56), channel_id=1, source_target_pairs={{0,5},{1,4},{2,7},{3,6},{4,1},{5,0},{6,3},{7,2},{8,13},{9,12},{10,... | collective-permute-start | bytes 3538952 | tf_op jit(solution)/shard_map/ppermute | solution.py:40
  144.6 58.7 %collective-permute-start.25 = (bf16[2,384,768]{2,1,0:T(8,128)(2,1)S(1)}, bf16[2,384,768]{2,1,0:T(8,128)(2,1)S(1)}, u32[]{:S(2)}, u32[]{:S(2)}) collective-permute-start(bf16[2,384,768]{2,1,0:T(8,128)(2,1)S(1)} %get-tuple-element.53), channel_id=1, source_target_pairs={{0,2},{1,3},{2,4},{3,5},{4,6},{5,7},{6,0},{7,1},{8,10},{9,11},{10,... | collective-permute-start | bytes 3538952 | tf_op jit(solution)/shard_map/ppermute | solution.py:40
  145.8 57.4 %collective-permute-start.29 = (bf16[2,384,768]{2,1,0:T(8,128)(2,1)S(1)}, bf16[2,384,768]{2,1,0:T(8,128)(2,1)S(1)}, u32[]{:S(2)}, u32[]{:S(2)}) collective-permute-start(bf16[2,384,768]{2,1,0:T(8,128)(2,1)S(1)} %get-tuple-element.57), channel_id=1, source_target_pairs={{0,6},{1,7},{2,0},{3,1},{4,2},{5,3},{6,4},{7,5},{8,14},{9,15},{10,... | collective-permute-start | bytes 3538952 | tf_op jit(solution)/shard_map/ppermute | solution.py:40
  152.0 51.2 %collective-permute-start.24 = (bf16[2,384,768]{2,1,0:T(8,128)(2,1)S(1)}, bf16[2,384,768]{2,1,0:T(8,128)(2,1)S(1)}, u32[]{:S(2)}, u32[]{:S(2)}) collective-permute-start(bf16[2,384,768]{2,1,0:T(8,128)(2,1)S(1)} %get-tuple-element.52), channel_id=1, source_target_pairs={{0,1},{1,0},{2,3},{3,2},{4,5},{5,4},{6,7},{7,6},{8,9},{9,8},{10,11... | collective-permute-start | bytes 3538952 | tf_op jit(solution)/shard_map/ppermute | solution.py:40
  152.3 76.3 %collective-permute-start.26 = (bf16[2,384,768]{2,1,0:T(8,128)(2,1)S(1)}, bf16[2,384,768]{2,1,0:T(8,128)(2,1)S(1)}, u32[]{:S(2)}, u32[]{:S(2)}) collective-permute-start(bf16[2,384,768]{2,1,0:T(8,128)(2,1)S(1)} %get-tuple-element.54), channel_id=1, source_target_pairs={{0,3},{1,2},{2,5},{3,4},{4,7},{5,6},{6,1},{7,0},{8,11},{9,10},{10,... | collective-permute-start | bytes 3538952 | tf_op jit(solution)/shard_map/ppermute | solution.py:40
  187.4 41.9 %collective-permute-start.30 = (bf16[2,384,768]{2,1,0:T(8,128)(2,1)S(1)}, bf16[2,384,768]{2,1,0:T(8,128)(2,1)S(1)}, u32[]{:S(2)}, u32[]{:S(2)}) collective-permute-start(bf16[2,384,768]{2,1,0:T(8,128)(2,1)S(1)} %get-tuple-element.58), channel_id=1, source_target_pairs={{0,7},{1,6},{2,1},{3,0},{4,3},{5,2},{6,5},{7,4},{8,15},{9,14},{10,... | collective-permute-start | bytes 3538952 | tf_op jit(solution)/shard_map/ppermute | solution.py:40
  233.2 10.8 %collective-permute-start.34 = (bf16[2,384,768]{2,1,0:T(8,128)(2,1)S(1)}, bf16[2,384,768]{2,1,0:T(8,128)(2,1)S(1)}, u32[]{:S(2)}, u32[]{:S(2)}) collective-permute-start(bf16[2,384,768]{2,1,0:T(8,128)(2,1)S(1)} %get-tuple-element.66), channel_id=1, source_target_pairs={{0,1},{1,0},{2,3},{3,2},{4,5},{5,4},{6,7},{7,6},{8,9},{9,8},{10,11... | collective-permute-start | bytes 3538952 | tf_op jit(solution)/shard_map/ppermute | solution.py:40
  236.5 6.4 %collective-permute-start.32 = (bf16[1,384,768]{2,1,0:T(8,128)(2,1)S(1)}, bf16[1,384,768]{2,1,0:T(8,128)(2,1)S(1)}, u32[]{:S(2)}, u32[]{:S(2)}) collective-permute-start(bf16[1,384,768]{2,1,0:T(8,128)(2,1)S(1)} %get-tuple-element.64), channel_id=1, source_target_pairs={{0,1},{1,0},{2,3},{3,2},{4,5},{5,4},{6,7},{7,6},{8,9},{9,8},{10,11... | collective-permute-start | bytes 1769480 | tf_op jit(solution)/shard_map/ppermute | solution.py:40
  242.8 4.8 %collective-permute-start.31 = (bf16[1,384,768]{2,1,0:T(8,128)(2,1)S(1)}, bf16[1,384,768]{2,1,0:T(8,128)(2,1)S(1)}, u32[]{:S(2)}, u32[]{:S(2)}) collective-permute-start(bf16[1,384,768]{2,1,0:T(8,128)(2,1)S(1)} %get-tuple-element.62), channel_id=1, source_target_pairs={{0,1},{1,0},{2,3},{3,2},{4,5},{5,4},{6,7},{7,6},{8,9},{9,8},{10,11... | collective-permute-start | bytes 1769480 | tf_op jit(solution)/shard_map/ppermute | solution.py:40
  243.1 16.0 %collective-permute-start.33 = (bf16[384,768]{1,0:T(8,128)(2,1)S(1)}, bf16[384,768]{1,0:T(8,128)(2,1)S(1)}, u32[]{:S(2)}, u32[]{:S(2)}) collective-permute-start(bf16[384,768]{1,0:T(8,128)(2,1)S(1)} %fusion), channel_id=1, source_target_pairs={{0,4},{1,5},{2,6},{3,7},{4,0},{5,1},{6,2},{7,3},{8,12},{9,13},{10,... | collective-permute-start | bytes 1769480 | tf_op jit(solution)/shard_map/ppermute | solution.py:40
  244.4 28.2 %collective-permute-start.35 = (bf16[384,768]{1,0:T(8,128)(2,1)S(1)}, bf16[384,768]{1,0:T(8,128)(2,1)S(1)}, u32[]{:S(2)}, u32[]{:S(2)}) collective-permute-start(bf16[384,768]{1,0:T(8,128)(2,1)S(1)} %get-tuple-element.71), channel_id=1, source_target_pairs={{0,2},{1,3},{2,4},{3,5},{4,6},{5,7},{6,0},{7,1},{8,10},{9,11},{10,... | collective-permute-start | bytes 1769480 | tf_op jit(solution)/shard_map/ppermute | solution.py:40
  246.3 26.3 %collective-permute-start.36 = (bf16[384,768]{1,0:T(8,128)(2,1)S(1)}, bf16[384,768]{1,0:T(8,128)(2,1)S(1)}, u32[]{:S(2)}, u32[]{:S(2)}) collective-permute-start(bf16[384,768]{1,0:T(8,128)(2,1)S(1)} %get-tuple-element.72), channel_id=1, source_target_pairs={{0,6},{1,7},{2,0},{3,1},{4,2},{5,3},{6,4},{7,5},{8,14},{9,15},{10,... | collective-permute-start | bytes 1769480 | tf_op jit(solution)/shard_map/ppermute | solution.py:40
